TPU v7x, 256 devices: a whole 4x4x8 slice. The times are simulated.
256 devices in a mesh: child: 2 (over core), row: 4 (over x), col: 32 (over y, z).
Axes of the slice: x: 4, y: 4, z: 8, core: 2. Of those that a mesh axis runs over, the one named last changes fastest.
Arguments:
- schur_blocks: bfloat16 [2, 16384, 16384], P('child', 'row', 'col'), may hold values from -2 to 2
- child_map: int32 [2, 16384], replicated, may hold values from 0 to 24575, as said below
- round_seeds: int32 [2], replicated, may hold values from 1 to 999999
Outputs:
- leaf_bases: float32 [24576, 256], P(('row', 'child', 'col'))
- fresh_samples: float32 [24576, 256], P(('row', 'child', 'col'))
Inputs may be any that keep to these rules, and one draw needn't show every extreme that they name: For each child c and each block r < 4, the entries child_map[c, r * 4096 : (r + 1) * 4096] rise strictly, lie in parent rows [r * 6144, (r + 1) * 6144), and include both ends of that range.
All inputs are finite; a program needn't handle non-finite values.
Results may differ from a plain program's by a relative error of at most 0.0031.
Values sent between devices are 32-bit elements; how exact they have to be, the bound alone decides.
A program may use at most 64 MiB of HBM per device.

v0:
```python
import jax
import jax.numpy as jnp
from jax import lax
from jax.sharding import PartitionSpec as P

NP = 24576
K = 256


def sample_rows(seed_value, parents, sample_width):
    hashed = (
        parents[:, None] * 40503
        + lax.iota(jnp.int32, sample_width)[None, :] * 9973
        + seed_value * 2654435
    )
    hashed = hashed ^ hashed >> 15 & 131071
    hashed = hashed * 73244475
    hashed = hashed ^ hashed >> 13 & 524287
    hashed = hashed * 1274126177
    hashed = hashed ^ hashed >> 16 & 65535
    unit_value = (hashed & 16777215).astype(jnp.float32) * (1.0 / 16777216.0)
    return (unit_value - 0.5) * 3.4641016


def body(schur_blocks, child_map, round_seeds):
    child_block = schur_blocks[0]
    block_rows, block_cols = child_block.shape
    child_count = lax.axis_size("child")
    col_count = lax.axis_size("col")
    row_count_axis = lax.axis_size("row")
    child_index = lax.axis_index("child")
    row_index = lax.axis_index("row")
    col_index = lax.axis_index("col")
    child_order = child_map.shape[1]
    own_map = lax.dynamic_index_in_dim(child_map, child_index, 0, keepdims=False)
    col_ids = lax.dynamic_slice_in_dim(own_map, col_index * block_cols, block_cols)
    leaf_rows = NP // row_count_axis
    own_rows = leaf_rows // (child_count * col_count)
    leaf_base = row_index * leaf_rows

    def sketch_rows(seed_list):
        samples = jnp.concatenate(
            [sample_rows(seed_value, col_ids, K) for seed_value in seed_list], axis=1
        ).astype(jnp.bfloat16)
        return jnp.dot(child_block, samples, preferred_element_type=jnp.float32)

    def extend(partial_value):
        summed = lax.psum_scatter(partial_value, "col", scatter_dimension=0, tiled=True)
        flat_map = child_map.reshape(-1)
        wanted = (
            leaf_base
            + (child_index * col_count + col_index) * own_rows
            + lax.iota(jnp.int32, own_rows)
        )
        shard_rows = lax.all_gather(summed, ("child", "col"), axis=0, tiled=True)
        gathered_pos = lax.iota(jnp.int32, shard_rows.shape[0])
        source = (
            gathered_pos // block_rows * child_order
            + row_index * block_rows
            + gathered_pos % block_rows
        )
        parent_ids = jnp.take(flat_map, source)
        select = (wanted[:, None] == parent_ids[None, :]).astype(jnp.float32)
        return jnp.dot(select, shard_rows, precision=lax.Precision.HIGHEST)

    first_leaf = extend(sketch_rows([round_seeds[0]]))
    second_leaf = extend(sketch_rows([round_seeds[1]]))
    gram_local = jnp.dot(first_leaf.T, first_leaf, precision=lax.Precision.HIGHEST)
    gram_matrix = lax.psum(gram_local, ("child", "col")) / leaf_rows
    lower_factor = jnp.linalg.cholesky(gram_matrix)
    leaf_basis = lax.linalg.triangular_solve(
        lower_factor, first_leaf, left_side=False, lower=True, transpose_a=True
    )
    coef_local = jnp.dot(leaf_basis.T, second_leaf, precision=lax.Precision.HIGHEST)
    coefficients = lax.psum(coef_local, ("child", "col")) / leaf_rows
    fresh_samples = second_leaf - jnp.dot(leaf_basis, coefficients, precision=lax.Precision.HIGHEST)
    return (leaf_basis, fresh_samples)


def solution(mesh):
    placed = (P("child", "row", "col"), P(), P())
    return jax.shard_map(
        body,
        mesh=mesh,
        in_specs=placed,
        out_specs=(P(("row", "child", "col"), None), P(("row", "child", "col"), None)),
        check_vma=False,
    )
```

profile of v0, /device:TPU:1, one launch (start us, length us, event | category | flops | bytes accessed | tf_op | source)
XLA Modules:
  0.0 1073.4 jit_solution(4717258641060240434)
XLA Ops:
  7.2 0.0 reduce-scatter.3.cloned.1.call-start
  7.2 1.3 fusion.102
  9.2 0.8 dynamic-slice_multiply_fusion
  9.9 5.7 convolution_bitcast_fusion.1
  15.6 0.0 reduce-scatter.3.cloned.1.call-update
  15.7 0.0 reduce-scatter.5.cloned.1.call-start
  16.3 5.7 convolution_bitcast_fusion
  22.1 0.0 reduce-scatter.5.cloned.1.call-update
  22.1 0.0 all-gather.3.cloned.1.call-start
  22.1 217.3 %reduce-scatter.3.cloned.1.call-done = f32[128,256]{0,1:T(8,128)} async-done(((f32[4096,256]{0,1:T(8,128)}), f32[128,256]{0,1:T(8,128)}) %reduce-scatter.3.cloned.1.call-update) | async-done | bytes 131088 | tf_op jit(solution)/shard_map/reduce_scatter | solution.py:48
  239.5 0.0 all-gather.3.cloned.1.call-update
  239.5 0.0 all-gather.5.cloned.1.call-start
  239.6 226.7 %reduce-scatter.5.cloned.1.call-done = f32[128,256]{0,1:T(8,128)} async-done(((f32[4096,256]{0,1:T(8,128)}), f32[128,256]{0,1:T(8,128)}) %reduce-scatter.5.cloned.1.call-update) | async-done | bytes 131088 | tf_op jit(solution)/shard_map/reduce_scatter | solution.py:48
  466.2 0.0 all-gather.5.cloned.1.call-update
  466.3 0.0 all-reduce.4.cloned.1.call-start
  466.4 45.5 %gather_fusion = s32[8192]{0:T(1024)S(1)} fusion(s32[32768]{0:T(1024)S(1)} %bitcast.52, s32[8192]{0:T(1024)S(1)} %broadcast_clamp_fusion), kind=kCustom, calls=%fused_computation.clone | custom fusion | bytes 98304 | tf_op jit(solution)/shard_map/jit(_take)/gather | solution.py:62
  512.0 45.2 %all-gather.3.cloned.1.call-done = f32[8192,256]{0,1:T(8,128)} async-done(((f32[128,256]{0,1:T(8,128)}), f32[8192,256]{0,1:T(8,128)}) %all-gather.3.cloned.1.call-update) | async-done | bytes 8388624 | tf_op jit(solution)/shard_map/all_gather | solution.py:55
  557.2 8.0 fusion.4
  565.2 1.1 fusion.103
  566.4 0.0 all-reduce.4.cloned.1.call-update
  566.4 0.2 all-reduce.6.cloned.1.call-start
  566.6 78.4 %all-gather.5.cloned.1.call-done = f32[8192,256]{0,1:T(8,128)} async-done(((f32[128,256]{0,1:T(8,128)}), f32[8192,256]{0,1:T(8,128)}) %all-gather.5.cloned.1.call-update) | async-done | bytes 8388624 | tf_op jit(solution)/shard_map/all_gather | solution.py:55
  645.0 8.0 fusion.2
  653.1 173.0 %all-reduce.4.cloned.1.call-done = f32[256,256]{0,1:T(8,128)} async-done(((f32[256,256]{0,1:T(8,128)}), f32[256,256]{0,1:T(8,128)}) %all-reduce.4.cloned.1.call-update) | async-done | bytes 262160 | tf_op jit(solution)/shard_map/psum | solution.py:69
  826.0 1.0 broadcast_multiply_fusion
  827.0 0.1 copy.8
  827.1 1.0 fusion.26
  828.2 11.7 %cholesky.50 = f32[128,128]{1,0:T(8,128)S(1)} custom-call(f32[128,128]{1,0:T(8,128)S(1)} %cholesky.118), custom_call_target="Cholesky" | custom-call | tf_op jit(solution)/shard_map/jit(cholesky)/cholesky | solution.py:70
  839.9 9.8 custom-call.14
  849.7 0.2 constant_dynamic-update-slice_fusion.1
  850.0 0.3 convolution_subtract_fusion.1
  850.2 11.9 %cholesky.105 = f32[128,128]{1,0:T(8,128)S(1)} custom-call(f32[128,128]{1,0:T(8,128)S(1)} %convolution_subtract_fusion.1), custom_call_target="Cholesky" | custom-call | tf_op jit(solution)/shard_map/jit(cholesky)/cholesky | solution.py:70
  862.2 0.7 compare_reduce_fusion
  864.2 0.1 triangular_solve.58
  864.2 3.9 while.1
  864.2 0.6 fusion.117
  864.8 1.3 bitcast_dynamic-update-slice_fusion.2
  866.2 0.6 fusion.117
  866.8 1.3 bitcast_dynamic-update-slice_fusion.2
  868.1 19.7 %custom-call.15 = f32[2,128,128]{1,2,0:T(8,128)S(1)} custom-call(f32[2,128,128]{2,1,0:T(8,128)S(1)} %get-tuple-element.10), custom_call_target="InvertDiagBlocksLowerTriangular" | custom-call | tf_op jit(solution)/shard_map/triangular_solve | solution.py:71
  887.8 0.2 fusion.61
  888.0 0.2 convolution_subtract_fusion.2
  888.3 0.2 fusion.59
  888.5 0.0 copy-start
  888.5 1.1 fusion.104
  889.6 0.0 all-reduce.6.cloned.1.call-update
  889.6 174.9 %all-reduce.6.cloned.1.call-done = f32[256,256]{0,1:T(8,128)} async-done(((f32[256,256]{0,1:T(8,128)}), f32[256,256]{0,1:T(8,128)}) %all-reduce.6.cloned.1.call-update) | async-done | bytes 262160 | tf_op jit(solution)/shard_map/psum | solution.py:75
  1064.6 2.0 convolution_subtract_fusion
  (18 shorter events, 0.2 us)
Async XLA Ops:
  7.2 232.3 %reduce-scatter.3.cloned.1.call-start = ((), (), s32[]{:S(2)}) async-start(), calls=%async_computation.2 | async-start | bytes 4325376 | tf_op jit(solution)/shard_map/reduce_scatter | solution.py:48
  15.7 450.6 %reduce-scatter.5.cloned.1.call-start = ((), (), s32[]{:S(2)}) async-start(), calls=%async_computation.5 | async-start | bytes 4325376 | tf_op jit(solution)/shard_map/reduce_scatter | solution.py:48
  22.1 444.3 %copy-start.1 = (s32[2,16384]{1,0:T(2,128)S(1)}, s32[2,16384]{1,0:T(2,128)}, u32[]{:S(2)}) copy-start(s32[2,16384]{1,0:T(2,128)} %param.6) | copy-start | bytes 393220
  22.1 535.1 %all-gather.3.cloned.1.call-start = ((), (), s32[]{:S(2)}) async-start(), calls=%async_computation.3 | async-start | bytes 8519680 | tf_op jit(solution)/shard_map/all_gather | solution.py:55
  239.5 405.5 %all-gather.5.cloned.1.call-start = ((), (), s32[]{:S(2)}) async-start(), calls=%async_computation.6 | async-start | bytes 8519680 | tf_op jit(solution)/shard_map/all_gather | solution.py:55
  466.3 359.8 %all-reduce.4.cloned.1.call-start = ((), (), s32[]{:S(2)}) async-start(), calls=%async_computation.4 | async-start | bytes 524288 | tf_op jit(solution)/shard_map/psum | solution.py:69
  566.4 498.2 %all-reduce.6.cloned.1.call-start = ((), (), s32[]{:S(2)}) async-start(), calls=%async_computation.7 | async-start | bytes 524288 | tf_op jit(solution)/shard_map/psum | solution.py:75
  888.5 178.0 %copy-start = (f32[96,256]{1,0:T(8,128)}, f32[96,256]{1,0:T(8,128)S(1)}, u32[]{:S(2)}) copy-start(f32[96,256]{1,0:T(8,128)S(1)} %pad_maximum_fusion) | copy-start | bytes 294916
Sparse Core Ops, SparseCore 0:
  15.8 223.6 reduce-scatter.2
  243.4 222.8 reduce-scatter.4
  468.8 88.3 all-gather.2
  559.6 85.3 all-gather.4
  648.4 177.6 all-reduce.3
  889.8 174.7 all-reduce.5
where the time goes:
time: 1070 us
  waiting for transfers between devices  916 us (86%)
  other arithmetic  56.7 us (5%)
  local copies, waits for them, and re-layouts  51 us (5%)
  matrix products  32.8 us (3%)
  between operations  16.9 us (2%)
    reduce_scatter x2, waiting for transfers between devices, extend(): lax.psum_scatter(partial_value, 'col', scatter_dimension=0, tiled=True)  444 us
    psum x1, waiting for transfers between devices, body(): coefficients = lax.psum(coef_local, ('child', 'col')) / leaf_rows  175 us
    psum x1, waiting for transfers between devices, body(): gram_matrix = lax.psum(gram_local, ('child', 'col')) / leaf_rows  173 us
    all_gather x2, waiting for transfers between devices, extend(): shard_rows = lax.all_gather(summed, ('child', 'col'), axis=0, tiled=True)  124 us
    gather x1, local copies, waits for them, and re-layouts, extend(): parent_ids = jnp.take(flat_map, source)  45.5 us
    another operation x6, other arithmetic, body(): lower_factor = jnp.linalg.cholesky(gram_matrix)  34.2 us
  transfers between devices with their start and end apart: 6, of which 6 were waited for; matrix products, arithmetic and copies ran while one was open for 6% of the time, Pallas kernels for 0%

commit v1 on v0

v1 whole, which is shorter than its diff:
```python
import functools
import jax
import jax.numpy as jnp
from jax import lax
from jax.experimental import pallas as pl
from jax.experimental.pallas import tpu as pltpu
from jax.sharding import PartitionSpec as P

K = 256
TILE = 128
STEP_TILES = 4
GRIDS = {32: (4, 8), 8: (4, 2), 4: (2, 2), 16: (4, 4)}
MESH = pl.DeviceIdType.MESH
HI = lax.Precision.HIGHEST
F32 = jnp.float32


def hash_values(ids_row, col, seed):
    h = ids_row * 40503 + col * 9973 + seed * 2654435
    h = h ^ ((h >> 15) & 131071)
    h = h * 73244475
    h = h ^ ((h >> 13) & 524287)
    h = h * 1274126177
    h = h ^ ((h >> 16) & 65535)
    unit = (h & 16777215).astype(F32) * (1.0 / 16777216.0)
    return (unit - 0.5) * 3.4641016


def sketch_kernel(base_ref, starts_ref, seeds_ref, ids_ref, map_ref, a_ref, out_ref, st_ref, e_ref):
    step = pl.program_id(0)
    cols = ids_ref.shape[1]

    @pl.when(step == 0)
    def _():
        ids = ids_ref[...]

        def draw(i, carry):
            j0 = pl.multiple_of(i * 32, 32)
            t = j0 // K
            col = lax.broadcasted_iota(jnp.int32, (32, cols), 0) + (j0 - t * K)
            st_ref[pl.ds(j0, 32), :] = hash_values(ids, col, seeds_ref[t]).astype(jnp.bfloat16)
            return carry

        lax.fori_loop(0, 2 * K // 32, draw, 0)

    for q in range(STEP_TILES):
        t = step * STEP_TILES + q
        b = starts_ref[t]
        window = jnp.concatenate([map_ref[pl.ds(b, 1), :], map_ref[pl.ds(b + 1, 1), :]], axis=1)
        wanted = lax.broadcasted_iota(jnp.int32, (TILE, 2 * TILE), 0) + (base_ref[0] + t * TILE)
        pick = jnp.where(window == wanted, 1.0, 0.0).astype(jnp.bfloat16)
        rows = a_ref[pl.ds(pl.multiple_of(b * TILE, TILE), 2 * TILE), :]
        e_ref[q * TILE:(q + 1) * TILE, :] = jnp.dot(
            pick, rows, preferred_element_type=F32
        ).astype(jnp.bfloat16)
    for half in range(2):
        out_ref[half] = lax.dot_general(
            e_ref[...], st_ref[half * K:(half + 1) * K, :], (((1,), (1,)), ((), ())),
            preferred_element_type=F32,
        )


def sketch(child_block, block_map, col_ids, seeds, leaf_base, leaf_rows):
    block_rows, block_cols = child_block.shape
    map2d = block_map.reshape(block_rows // TILE, TILE)
    tiles = leaf_rows // TILE
    firsts = leaf_base + lax.iota(jnp.int32, tiles) * TILE
    starts = jnp.sum((map2d[:, TILE - 1][None, :] < firsts[:, None]).astype(jnp.int32), axis=1)
    starts = jnp.minimum(starts, block_rows // TILE - 2)
    rows = STEP_TILES * TILE
    smem = pl.BlockSpec(memory_space=pltpu.SMEM)
    return pl.pallas_call(
        sketch_kernel,
        grid=(leaf_rows // rows,),
        out_shape=jax.ShapeDtypeStruct((2, leaf_rows, K), F32),
        in_specs=[
            smem, smem, smem,
            pl.BlockSpec((1, block_cols), lambda i: (0, 0)),
            pl.BlockSpec(map2d.shape, lambda i: (0, 0)),
            pl.BlockSpec((block_rows, block_cols), lambda i: (0, 0)),
        ],
        out_specs=pl.BlockSpec((2, rows, K), lambda i: (0, i, 0)),
        scratch_shapes=[
            pltpu.VMEM((2 * K, block_cols), jnp.bfloat16),
            pltpu.VMEM((rows, block_cols), jnp.bfloat16),
        ],
        compiler_params=pltpu.CompilerParams(vmem_limit_bytes=40 << 20),
    )(leaf_base.reshape(1), starts, seeds, col_ids.reshape(1, block_cols), map2d, child_block)


def row_sets(rows):
    if rows == 96:
        return [("Y", 0, 32, 0), ("Z", 32, 16, 0), ("Y", 48, 24, 1), ("Z", 72, 24, 1)]
    q = rows // 4
    return [("Y", 0, q, 0), ("Z", q, q, 0), ("Y", 2 * q, q, 1), ("Z", 3 * q, q, 1)]


def hops(n, orient):
    long, short = n // 2, n - 1 - n // 2
    return (short, long) if orient else (long, short)


def reduce_kernel(ny, nz, rows, p_ref, y_ref, g_ref, *refs):
    sets = row_sets(rows)
    nsets = len(sets)
    h_ref, r_ref = refs[0], refs[1]
    slots1 = refs[2:2 + nsets]
    slots2 = refs[2 + nsets:2 + 2 * nsets]
    (ypad, gloc, gpart, gz, zr, gs, yr, gf,
     load_sem, xs, xr, s1, q1, s2, q2, as_, ar_) = refs[2 + 2 * nsets:]

    c = lax.axis_index("child")
    k = lax.axis_index("col")
    my_y = k // nz
    my_z = k - my_y * nz
    other = 1 - c

    def at_y(y):
        return {"col": y * nz + my_z}

    def at_z(z):
        return {"col": my_y * nz + z}

    pending = []

    def put(src, dst, ssem, rsem, dev):
        cp = pltpu.make_async_remote_copy(
            src_ref=src, dst_ref=dst, send_sem=ssem, recv_sem=rsem,
            device_id=dev, device_id_type=MESH)
        cp.start()
        pending.append(cp)
        return cp

    loads = []
    for h in range(2):
        cp = pltpu.make_async_copy(p_ref.at[h, c], h_ref.at[h], load_sem.at[h])
        cp.start()
        loads.append(cp)

    barrier = pltpu.get_barrier_semaphore()
    peers = [{"child": other}]
    peers += [at_y(lax.rem(my_y + j, ny)) for j in range(1, ny)]
    peers += [at_z(lax.rem(my_z + j, nz)) for j in range(1, nz)]
    for dev in peers:
        pl.semaphore_signal(barrier, inc=1, device_id=dev, device_id_type=MESH)
    pl.semaphore_wait(barrier, len(peers))

    swaps = {}
    for h in range(2):
        for i, (_, r0, nr, _) in enumerate(sets):
            swaps[h, i] = put(
                p_ref.at[h, other, :, :, pl.ds(r0, nr), :],
                r_ref.at[h, :, :, pl.ds(r0, nr), :],
                xs.at[h, i], xr.at[h, i], {"child": other})

    class Ring:
        def __init__(self, n, pos, at, orient, own, own_ix, lead, slot, slot_ix, ssem, rsem):
            self.n, self.pos, self.at = n, pos, at
            self.hp, self.hm = hops(n, orient)
            self.own, self.own_ix, self.lead = own, own_ix, lead
            self.slot, self.slot_ix, self.ssem, self.rsem = slot, slot_ix, ssem, rsem
            self.copies = {}

        def send(self, sign, s):
            n, reach = self.n, self.hp if sign > 0 else self.hm
            base = 0 if sign > 0 else self.hp
            d = lax.rem(self.pos + sign * (reach - s) + n, n)
            dev = self.at(lax.rem(self.pos + sign + n, n))
            if s:
                self.add(base + s - 1, d)
            src = self.slot(base + s - 1) if s else self.own(d)
            m = base + s
            self.copies[m] = put(src, self.slot(m), self.ssem(m), self.rsem(m), dev)

        def add(self, m, d):
            ref, ix = self.slot_ix
            own, oix = self.own_ix
            self.copies[m].wait_recv()

            def body(i, carry):
                ref[ix(m, i)] = ref[ix(m, i)] + own[oix(d, i)]
                return carry
            lax.fori_loop(0, self.lead, body, 0)

        def turn(self, s):
            if s < self.hp:
                self.send(1, s)
            if s < self.hm:
                self.send(-1, s)

        @property
        def turns(self):
            return max(self.hp, self.hm)

        def finish(self):
            ref, ix = self.slot_ix
            own, oix = self.own_ix
            last = [m for m, ok in ((self.hp - 1, self.hp), (self.hp + self.hm - 1, self.hm)) if ok]
            for m in last:
                self.copies[m].wait_recv()

            def body(i, carry):
                total = own[oix(self.pos, i)]
                for m in last:
                    total = total + ref[ix(m, i)]
                own[oix(self.pos, i)] = total
                return carry
            lax.fori_loop(0, self.lead, body, 0)

    def flow(h, i):
        color, r0, nr, orient = sets[i]
        rs = pl.ds(r0, nr)
        sl1, sl2 = slots1[i], slots2[i]
        sems = (lambda m: s1.at[h, i, m], lambda m: q1.at[h, i, m])
        sems2 = (lambda m: s2.at[h, i, m], lambda m: q2.at[h, i, m])
        ring1 = (lambda m: sl1.at[h, m], (sl1, lambda m, j: (h, m, j)))
        ring2 = (lambda m: sl2.at[h, m], (sl2, lambda m, j: (h, m, j)))
        if color == "Y":
            first = Ring(ny, my_y, at_y, orient,
                         lambda d: h_ref.at[h, d, :, rs, :],
                         (h_ref, lambda d, j: (h, d, j, rs, slice(None))), nz,
                         *ring1, *sems)
            second = Ring(nz, my_z, at_z, orient,
                          lambda d: h_ref.at[h, my_y, pl.ds(d, 1), rs, :],
                          (h_ref, lambda d, j: (h, my_y, d, rs, slice(None))), 1,
                          *ring2, *sems2)
        else:
            first = Ring(nz, my_z, at_z, orient,
                         lambda d: h_ref.at[h, :, d, rs, :],
                         (h_ref, lambda d, j: (h, j, d, rs, slice(None))), ny,
                         *ring1, *sems)
            second = Ring(ny, my_y, at_y, orient,
                          lambda d: h_ref.at[h, pl.ds(d, 1), my_z, rs, :],
                          (h_ref, lambda d, j: (h, d, my_z, rs, slice(None))), 1,
                          *ring2, *sems2)

        def begin():
            swaps[h, i].wait_recv()

            def body(y, carry):
                for z in range(nz):
                    ix = (h, y, z, rs, slice(None))
                    h_ref[ix] = h_ref[ix] + r_ref[ix]
                return carry
            lax.fori_loop(0, ny, body, 0)
            first.turn(0)

        def middle():
            first.finish()
            second.turn(0)

        acts = [begin]
        acts += [functools.partial(first.turn, s) for s in range(1, first.turns)]
        acts += [middle]
        acts += [functools.partial(second.turn, s) for s in range(1, second.turns)]
        acts += [second.finish]
        unit1, unit2 = (4.0, 2.0) if color == "Y" else (2.0, 2.0)
        times, t = [], h * 4.0 + 0.1 * i
        for a in range(len(acts)):
            times.append(t)
            t += unit1 if a < first.turns else unit2
        return list(zip(times, acts))

    for cp in loads:
        cp.wait()
    order = []
    for h in range(2):
        for i in range(nsets):
            order += flow(h, i)
    order.sort(key=lambda e: e[0])
    for _, act in order:
        act()

    ypad[...] = jnp.zeros_like(ypad)
    for h in range(2):
        ypad[0:rows, h * K:(h + 1) * K] = h_ref[h, my_y, my_z]
        y_ref[h] = h_ref[h, my_y, my_z]
    first_t = jnp.transpose(ypad[:, 0:K])
    gloc[...] = jnp.dot(first_t, ypad[...], precision=HI, preferred_element_type=F32).reshape(gloc.shape)

    cp = put(gloc.at[other], gpart, as_.at[0], ar_.at[0], {"child": other})
    cp.wait_recv()
    half = gloc[c] + gpart[...]
    gz[...] = half.reshape(gz.shape)
    got = []
    for j in range(1, nz):
        z = lax.rem(my_z + j, nz)
        got.append(put(gz.at[z], zr.at[j - 1], as_.at[j], ar_.at[j], at_z(z)))
    total = gz[my_z]
    for j in range(1, nz):
        got[j - 1].wait_recv()
        total = total + zr[j - 1]
    gs[...] = total
    got = []
    for j in range(1, ny):
        y = lax.rem(my_y + j, ny)
        got.append(put(gs, yr.at[j - 1], as_.at[nz + j - 1], ar_.at[nz + j - 1], at_y(y)))
    for j in range(1, ny):
        got[j - 1].wait_recv()
        total = total + yr[j - 1]
    gf[c, my_z] = total
    off = nz + ny - 1
    got = []
    for j in range(1, nz):
        z = lax.rem(my_z + j, nz)
        got.append(put(gf.at[c, my_z], gf.at[c, my_z], as_.at[off + j], ar_.at[off + j], at_z(z)))
    off2 = off + nz
    gave = [put(gf.at[c, my_z], gf.at[c, my_z], as_.at[off2], ar_.at[off2], {"child": other})]
    for j in range(1, nz):
        got[j - 1].wait_recv()
        z = lax.rem(my_z - j + nz, nz)
        gave.append(put(gf.at[c, z], gf.at[c, z], as_.at[off2 + j], ar_.at[off2 + j], {"child": other}))
    for cp in gave:
        cp.wait_recv()
    g_ref[...] = gf[...].reshape(g_ref.shape)
    for cp in pending:
        cp.wait_send()


def reduce_sketch(partial, ny, nz, rows):
    sets = row_sets(rows)
    cols = ny * nz
    shaped = partial.reshape(2, 2, ny, nz, rows, K)
    vm = pltpu.VMEM
    slots1 = [vm((2, (ny if s[0] == "Y" else nz) - 1, nz if s[0] == "Y" else ny, s[2], K), F32) for s in sets]
    slots2 = [vm((2, (nz if s[0] == "Y" else ny) - 1, 1, s[2], K), F32) for s in sets]
    dma = pltpu.SemaphoreType.DMA
    most = max(ny, nz) - 1
    piece = K // 2 // nz
    n_ar = 3 * nz + ny - 1
    return pl.pallas_call(
        functools.partial(reduce_kernel, ny, nz, rows),
        out_shape=(
            jax.ShapeDtypeStruct((2, rows, K), F32),
            jax.ShapeDtypeStruct((K, 2 * K), F32),
        ),
        in_specs=[pl.BlockSpec(memory_space=pl.ANY)],
        out_specs=[pl.BlockSpec(memory_space=pltpu.VMEM)] * 2,
        scratch_shapes=[
            vm((2, ny, nz, rows, K), F32), vm((2, ny, nz, rows, K), F32),
            *slots1, *slots2,
            vm((128, 2 * K), F32), vm((2, K // 2, 2 * K), F32), vm((K // 2, 2 * K), F32),
            vm((nz, piece, 2 * K), F32), vm((nz - 1, piece, 2 * K), F32), vm((piece, 2 * K), F32),
            vm((ny - 1, piece, 2 * K), F32), vm((2, nz, piece, 2 * K), F32),
            dma((2,)), dma((2, 4)), dma((2, 4)),
            dma((2, 4, most)), dma((2, 4, most)), dma((2, 4, most)), dma((2, 4, most)),
            dma((n_ar,)), dma((n_ar,)),
        ],
        compiler_params=pltpu.CompilerParams(
            collective_id=0, has_side_effects=True, vmem_limit_bytes=48 << 20),
    )(shaped)


BLK = 64


def solve_kernel(scale, y_ref, g_ref, q_ref, f_ref, aug_ref):
    rows = y_ref.shape[1]
    aug_ref[:, 0:K] = g_ref[:, 0:K] * scale
    aug_ref[:, K:2 * K] = g_ref[:, K:2 * K] * scale
    y1 = jnp.concatenate([y_ref[0], jnp.zeros((128 - rows, K), F32)], axis=0)
    aug_ref[:, 2 * K:2 * K + 128] = jnp.transpose(y1)
    sub = lax.broadcasted_iota(jnp.int32, (BLK, BLK), 0)
    lane = lax.broadcasted_iota(jnp.int32, (BLK, BLK), 1)
    for b in range(K // BLK):
        lo, hi = b * BLK, (b + 1) * BLK
        d = aug_ref[lo:hi, lo:hi]
        inv = jnp.where(sub == lane, 1.0, 0.0)
        for j in range(BLK):
            row = d[j:j + 1, :]
            factor = d[:, j:j + 1] * (1.0 / row[:, j:j + 1])
            factor = jnp.where(sub[:, 0:1] > j, factor, 0.0)
            irow = inv[j:j + 1, :]
            d = d - factor * row
            inv = inv - factor * irow
        pivots = jnp.sum(jnp.where(sub == lane, d, 0.0), axis=1, keepdims=True)
        inv = inv * (1.0 / jnp.sqrt(pivots))
        z = jnp.dot(inv, aug_ref[lo:hi, :], precision=HI, preferred_element_type=F32)
        aug_ref[lo:hi, :] = z
        if hi < K:
            u = jnp.transpose(aug_ref[lo:hi, hi // 128 * 128:K])
            u = u[hi - hi // 128 * 128:, :]
            aug_ref[hi:K, :] = aug_ref[hi:K, :] - jnp.dot(
                u, z, precision=HI, preferred_element_type=F32)
    basis = jnp.transpose(aug_ref[:, 2 * K:2 * K + 128])
    coef = aug_ref[:, K:2 * K]
    fit = jnp.dot(basis, coef, precision=HI, preferred_element_type=F32)
    q_ref[...] = basis[0:rows, :]
    f_ref[...] = y_ref[1] - fit[0:rows, :]


def solve(sketch_rows, grams, leaf_rows):
    rows = sketch_rows.shape[1]
    out = jax.ShapeDtypeStruct((rows, K), F32)
    return pl.pallas_call(
        functools.partial(solve_kernel, 1.0 / leaf_rows),
        out_shape=(out, out),
        in_specs=[pl.BlockSpec(memory_space=pltpu.VMEM)] * 2,
        out_specs=[pl.BlockSpec(memory_space=pltpu.VMEM)] * 2,
        scratch_shapes=[pltpu.VMEM((K, 2 * K + 128), F32)],
    )(sketch_rows, grams)


def make_body(parent_rows):
    def body(schur_blocks, child_map, round_seeds):
        child_block = schur_blocks[0]
        block_rows, block_cols = child_block.shape
        col_count = lax.axis_size("col")
        ny, nz = GRIDS[col_count]
        row_count = lax.axis_size("row")
        child, row, col = (lax.axis_index(a) for a in ("child", "row", "col"))
        leaf_rows = parent_rows // row_count
        own_rows = leaf_rows // (2 * col_count)
        own_map = lax.dynamic_index_in_dim(child_map, child, 0, keepdims=False)
        col_ids = lax.dynamic_slice_in_dim(own_map, col * block_cols, block_cols)
        block_map = lax.dynamic_slice_in_dim(own_map, row * block_rows, block_rows)
        partial = sketch(child_block, block_map, col_ids, round_seeds, row * leaf_rows, leaf_rows)
        y, g = reduce_sketch(partial, ny, nz, own_rows)
        return solve(y, g, leaf_rows)
    return body


def solution(mesh, parent_rows=24576):
    placed = (P("child", "row", "col"), P(), P())
    return jax.shard_map(
        make_body(parent_rows),
        mesh=mesh,
        in_specs=placed,
        out_specs=(P(("row", "child", "col"), None), P(("row", "child", "col"), None)),
        check_vma=False,
    )
```

time: 1070 us -> 133 us (0.12)
  waiting for transfers between devices: 916 us -> 0 us
  Pallas kernels: 0 us -> 126 us
  other arithmetic: 56.7 us -> 0.1 us
  local copies, waits for them, and re-layouts: 51 us -> 6.1 us
  matrix products: 32.8 us -> 0 us
  between operations: 16.9 us -> 0.71 us
    reduce_scatter x2 -> x0, waiting for transfers between devices: 444 us -> none  [extend(): lax.psum_scatter(partial_value, 'col', scatter_dimension=0, tiled=True)]
    psum x2 -> x0, waiting for transfers between devices: 348 us -> none  [the longest x1 175 us: body(): coefficients = lax.psum(coef_local, ('child', 'col')) / leaf_rows]
    pallas_call x0 -> x3, Pallas kernels: none -> 126 us  [the longest x1 88.1 us: reduce_sketch(): pl.pallas_call(functools.partial(reduce_kernel, ny, nz, rows), out_shape=...]
    all_gather x2 -> x0, waiting for transfers between devices: 124 us -> none  [extend(): shard_rows = lax.all_gather(summed, ('child', 'col'), axis=0, tiled=True)]
    another operation x10 -> x0, other arithmetic: 53.9 us -> none  [the longest x6 34.2 us: body(): lower_factor = jnp.linalg.cholesky(gram_matrix)]
    gather x1 -> x0, local copies, waits for them, and re-layouts: 45.5 us -> none  [extend(): parent_ids = jnp.take(flat_map, source)]
    dot_general x7 -> x0, matrix products: 31.7 us -> none  [the longest x2 16 us: extend(): return jnp.dot(select, shard_rows, precision=lax.Precision.HIGHEST)]
  transfers between devices with their start and end apart: 6 -> 0, of which waited for: 6 -> 0; matrix products, arithmetic and copies ran while one was open for 6% -> 0% of each run, Pallas kernels for 0% -> 0%
where the time goes in v1:
time: 133 us
  Pallas kernels  126 us (95%)
  local copies, waits for them, and re-layouts  6.1 us (5%)
    pallas_call x1, Pallas kernels, reduce_sketch(): pl.pallas_call(functools.partial(reduce_kernel, ny, nz, rows), out_shape=...  88.1 us
    pallas_call x1, Pallas kernels, solve(): pl.pallas_call(functools.partial(solve_kernel, 1.0 / leaf_rows), out_shap...  25.7 us
    pallas_call x1, Pallas kernels, sketch(): pl.pallas_call(sketch_kernel, grid=(leaf_rows // rows,), out_shape=jax.Sh...  12 us
    unnamed x8, local copies, waits for them, and re-layouts  4.29 us

profile of v1, /device:TPU:1, one launch (start us, length us, event | category | flops | bytes accessed | tf_op | source)
XLA Modules:
  0.0 132.7 jit_solution(2192627586401249684)
XLA Ops:
  0.7 0.8 dynamic_slice.9.ids_ref
  1.4 0.9 dynamic_slice.8
  2.3 0.2 slice_reduce_fusion
  2.5 0.1 convert_reduce_fusion
  2.6 0.0 copy-start
  2.6 2.2 %copy-done = bf16[1,4096,512]{2,1,0:T(8,128)(2,1)S(1)} copy-done((bf16[1,4096,512]{2,1,0:T(8,128)(2,1)S(1)}, bf16[1,4096,512]{2,1,0:T(8,128)(2,1)}, u32[]{:S(2)}) %copy-start) | copy-done | bytes 4194328
  4.8 0.0 copy-start.3
  4.8 0.7 copy-done.3
  5.4 12.0 %shard_map.50 = f32[2,6144,256]{2,1,0:T(8,128)} custom-call(s32[1]{0:T(128)} %bitcast.base_ref, s32[48]{0:T(128)S(1)} %broadcast_minimum_fusion.starts_ref, s32[2]{0:T(128)S(1)} %copy-done.3, s32[1,512]{1,0:T(1,128)S(1)} %dynamic_slice.9.ids_ref, s32[32,128]{1,0:T(8,128)S(1)} %bitcast.6, bf16[4096,512]{1,0:T(8,128)(2,1)S(1)} %bitcast.4), custom_call_target="tpu_custom_call" | custom-call | tf_op jit(solution)/shard_map/pallas_call | solution.py:72
  17.4 88.1 %shard_map.51 = (f32[2,96,256]{2,1,0:T(8,128)S(1)}, f32[256,512]{1,0:T(8,128)S(1)}) custom-call(f32[2,2,4,8,96,256]{5,4,3,2,1,0:T(8,128)} %bitcast.7), custom_call_target="tpu_custom_call" | custom-call | tf_op jit(solution)/shard_map/pallas_call | solution.py:331
  105.6 0.0 copy-start.1
  105.6 0.8 copy-done.1
  106.4 0.0 copy-start.2
  106.4 0.7 copy-done.2
  107.0 25.7 %shard_map.52 = (f32[96,256]{1,0:T(8,128)}, f32[96,256]{1,0:T(8,128)}) custom-call(f32[2,96,256]{2,1,0:T(8,128)} %copy-done.2, f32[256,512]{1,0:T(8,128)} %copy-done.1), custom_call_target="tpu_custom_call" | custom-call | tf_op jit(solution)/shard_map/pallas_call | solution.py:395
  (2 shorter events, 0.0 us)
Async XLA Ops:
  2.6 2.2 %copy-start = (bf16[1,4096,512]{2,1,0:T(8,128)(2,1)S(1)}, bf16[1,4096,512]{2,1,0:T(8,128)(2,1)}, u32[]{:S(2)}) copy-start(bf16[1,4096,512]{2,1,0:T(8,128)(2,1)} %param.3) | copy-start | bytes 12582916
  4.8 0.7 copy-start.3
  105.6 0.8 copy-start.1
  106.4 0.7 copy-start.2

commit v2 on v0

v2 whole, which is shorter than its diff:
```python
import functools
import jax
import jax.numpy as jnp
from jax import lax
from jax.experimental import pallas as pl
from jax.experimental.pallas import tpu as pltpu
from jax.sharding import PartitionSpec as P

K = 256
TILE = 128
BLK = 32
GRIDS = {32: (4, 8), 8: (2, 4)}
MESH = pl.DeviceIdType.MESH
HI = lax.Precision.HIGHEST
F32 = jnp.float32
RATE = 46.0e3
HOP = 0.75
BASE = 1.0


def mm(a, b):
    return jnp.dot(a, b, precision=HI, preferred_element_type=F32)


def hash_values(ids_row, col, seed):
    h = ids_row * 40503 + col * 9973 + seed * 2654435
    h = h ^ ((h >> 15) & 131071)
    h = h * 73244475
    h = h ^ ((h >> 13) & 524287)
    h = h * 1274126177
    h = h ^ ((h >> 16) & 65535)
    unit = (h & 16777215).astype(F32) * (1.0 / 16777216.0)
    return (unit - 0.5) * 3.4641016


def row_sets(rows):
    if rows == 96:
        return [("Y", 0, 32, 0), ("Z", 32, 16, 0), ("Y", 48, 24, 1), ("Z", 72, 24, 1)]
    q = rows // 4
    return [("Y", 0, q, 0), ("Z", q, q, 0), ("Y", 2 * q, q, 1), ("Z", 3 * q, q, 1)]


def hops(n, orient):
    long, short = n // 2, n - 1 - n // 2
    return (short, long) if orient else (long, short)


class Act:
    def __init__(self, name, run, after=(), deps=(), sends=(), cost=0.15, idle=False, prio=0):
        self.name, self.run, self.after, self.deps = name, run, list(after), list(deps)
        self.sends, self.cost, self.idle, self.prio = list(sends), cost, idle, prio


def arrange(acts, now, arrive):
    arrive, free, done, order = dict(arrive), {}, set(), []
    left = list(acts)
    while left:
        ready = []
        for a in left:
            if all(n in done for n in a.after) and all(d in arrive for d in a.deps):
                ready.append((max([now] + [arrive[d] for d in a.deps]), a.prio, len(ready), a))
        work = [r for r in ready if not r[3].idle]
        spare = [r for r in ready if r[3].idle]
        pick = min(work or spare, key=lambda r: r[:3])
        if work and spare:
            s = min(spare, key=lambda r: r[:3])
            if s[0] + 0.6 * s[3].cost <= pick[0]:
                pick = s
        a = pick[3]
        now = pick[0] + a.cost
        for key, link, size, lag in a.sends:
            free[link] = max(free.get(link, 0.0), now) + size
            arrive[key] = free[link] + lag
        done.add(a.name)
        left.remove(a)
        order.append((now, a))
    return order


STEP_TILES = 4


def expand_kernel(map_ref, a_hbm, e_ref, a_ref, m2_ref, sv_ref, ss_ref, a_sem, sv_sem):
    step = pl.program_id(0)
    block_rows = a_ref.shape[0]
    blocks = block_rows // TILE
    c = lax.axis_index("child")
    row = lax.axis_index("row")
    base = row * (e_ref.shape[0] * pl.num_programs(0))

    @pl.when(step == 0)
    def _():
        load = pltpu.make_async_copy(a_hbm, a_ref, a_sem)
        load.start()

        def fill(j, carry):
            at = pl.multiple_of(row * block_rows + j * TILE, TILE)
            both = map_ref[:, pl.ds(at, TILE)]
            m2_ref[pl.ds(j, 1), :] = jnp.where(c == 0, both[0:1, :], both[1:2, :])
            return carry
        lax.fori_loop(0, blocks, fill, 0)
        firsts = base + lax.broadcasted_iota(jnp.int32, (blocks, TILE), 1) * TILE
        below = (m2_ref[:, TILE - 1:TILE] < firsts).astype(jnp.int32)
        counts = jnp.minimum(jnp.sum(below, axis=0, keepdims=True), blocks - 2)
        sv_ref[...] = jnp.broadcast_to(counts, sv_ref.shape)
        to_scalar = pltpu.make_async_copy(sv_ref, ss_ref, sv_sem)
        to_scalar.start()
        to_scalar.wait()
        load.wait()

    for q in range(STEP_TILES):
        t = step * STEP_TILES + q
        b = ss_ref[0, t]
        window = jnp.concatenate([m2_ref[pl.ds(b, 1), :], m2_ref[pl.ds(b + 1, 1), :]], axis=1)
        wanted = lax.broadcasted_iota(jnp.int32, (TILE, 2 * TILE), 0) + (base + t * TILE)
        pick = jnp.where(window == wanted, 1.0, 0.0).astype(jnp.bfloat16)
        src = a_ref[pl.ds(pl.multiple_of(b * TILE, TILE), 2 * TILE), :]
        e_ref[q * TILE:(q + 1) * TILE, :] = jnp.dot(
            pick, src, preferred_element_type=F32).astype(jnp.bfloat16)


def expand_rows(child_block, child_map, leaf_rows):
    block_rows, block_cols = child_block.shape
    bf = jnp.bfloat16
    rows = STEP_TILES * TILE
    return pl.pallas_call(
        expand_kernel,
        grid=(leaf_rows // rows,),
        out_shape=jax.ShapeDtypeStruct((leaf_rows, block_cols), bf),
        in_specs=[pl.BlockSpec(child_map.shape, lambda i: (0, 0)), pl.BlockSpec(memory_space=pl.ANY)],
        out_specs=pl.BlockSpec((rows, block_cols), lambda i: (i, 0)),
        scratch_shapes=[
            pltpu.VMEM((block_rows, block_cols), bf),
            pltpu.VMEM((block_rows // TILE, TILE), jnp.int32), pltpu.VMEM((8, TILE), jnp.int32),
            pltpu.SMEM((8, TILE), jnp.int32),
            pltpu.SemaphoreType.DMA(()), pltpu.SemaphoreType.DMA(()),
        ],
        compiler_params=pltpu.CompilerParams(vmem_limit_bytes=40 << 20),
    )(child_map, child_block)


def fused_kernel(ny, nz, rows, scale, seeds_ref, map_ref, e_hbm, q_ref, f_ref, *refs):
    sets = row_sets(rows)
    nsets = len(sets)
    slots1, slots2 = refs[:nsets], refs[nsets:2 * nsets]
    (st_ref, eo_ref, em_ref, xb_ref, h_ref, r_ref,
     ypad, gloc, gpart, gz, zr, gs, yr, gf, aug_ref, qw_ref,
     e_sem, xs, xr, s1, q1, s2, q2, as_, ar_) = refs[2 * nsets:]

    block_cols = em_ref.shape[2]

    c = lax.axis_index("child")
    k = lax.axis_index("col")
    my_y = k // nz
    my_z = k - my_y * nz
    other = 1 - c

    def at_y(y):
        return {"col": y * nz + my_z}

    def at_z(z):
        return {"col": my_y * nz + z}

    pending = []

    def remote(src, dst, ssem, rsem, dev):
        return pltpu.make_async_remote_copy(
            src_ref=src, dst_ref=dst, send_sem=ssem, recv_sem=rsem,
            device_id=dev, device_id_type=MESH)

    def put(*args):
        cp = remote(*args)
        cp.start()
        pending.append(cp)
        return cp

    def y_of(j):
        return lax.rem(my_y + ny // 2 - j + ny, ny)

    def fetch(side, j):
        half, dst = ((other, eo_ref), (c, em_ref))[side]
        return pltpu.make_async_copy(e_hbm.at[half, y_of(j)], dst.at[j], e_sem.at[side, j])

    for side in range(2):
        for j in range(ny):
            fetch(side, j).start()
    barrier = pltpu.get_barrier_semaphore()
    peers = [{"child": other}]
    peers += [at_y(lax.rem(my_y + j, ny)) for j in range(1, ny)]
    peers += [at_z(lax.rem(my_z + j, nz)) for j in range(1, nz)]
    for dev in peers:
        pl.semaphore_signal(barrier, inc=1, device_id=dev, device_id_type=MESH)

    both_ids = map_ref[:, pl.ds(pl.multiple_of(k * block_cols, TILE), block_cols)]
    ids = jnp.where(c == 0, both_ids[0:1, :], both_ids[1:2, :])

    def draw(i, carry):
        j0 = pl.multiple_of(i * 32, 32)
        t = j0 // K
        col = lax.broadcasted_iota(jnp.int32, (32, block_cols), 0) + (j0 - t * K)
        st_ref[pl.ds(j0, 32), :] = hash_values(ids, col, seeds_ref[t]).astype(jnp.bfloat16)
        return carry
    lax.fori_loop(0, 2 * K // 32, draw, 0)
    ypad[...] = jnp.zeros_like(ypad)

    def sketch(e, h):
        return lax.dot_general(
            e[...], st_ref[h * K:(h + 1) * K, :], (((1,), (1,)), ((), ())),
            preferred_element_type=F32).reshape(nz, rows, K)

    def swap(h, j):
        y = y_of(j)
        return remote(xb_ref.at[h, y], r_ref.at[h, y], xs.at[h, j], xr.at[h, j], {"child": other})

    pl.semaphore_wait(barrier, len(peers))

    def give0(j, carry):
        y = y_of(j)
        fetch(0, j).wait()
        xb_ref[0, y] = sketch(eo_ref.at[j], 0)
        swap(0, j).start()
        return carry
    lax.fori_loop(0, ny, give0, 0)

    def give1(j, carry):
        xb_ref[1, y_of(j)] = sketch(eo_ref.at[j], 1)
        swap(1, j).start()
        return carry
    lax.fori_loop(0, ny, give1, 0)

    def keep(j, carry):
        y = y_of(j)
        fetch(1, j).wait()
        h_ref[0, y] = sketch(em_ref.at[j], 0)
        h_ref[1, y] = sketch(em_ref.at[j], 1)
        return carry
    lax.fori_loop(0, ny, keep, 0)

    acts = []
    arrive = {("x", h, j): 4.5 + 1.7 * (j + 1 + ny * h) for h in range(2) for j in range(ny)}

    def presum(h, j):
        def run():
            swap(h, j).wait_recv()
            y = y_of(j)

            def body(z, carry):
                h_ref[h, y, z] = h_ref[h, y, z] + r_ref[h, y, z]
                return carry
            lax.fori_loop(0, nz, body, 0)
        acts.append(Act(("pre", h, j), run, deps=[("x", h, j)], cost=0.3, prio=h))

    class Ring:
        def __init__(self, tag, axis, n, pos, at, orient, own, own_ix, lead, slot, ssem, rsem, nr):
            self.tag, self.axis, self.n, self.pos, self.at = tag, axis, n, pos, at
            self.hp, self.hm = hops(n, orient)
            self.own, self.own_ix, self.lead = own, own_ix, lead
            self.slot, self.ssem, self.rsem = slot, ssem, rsem
            self.size = lead * nr * K * 4
            self.copies = {}

        def reach(self, sign):
            return self.hp if sign > 0 else self.hm

        def index(self, sign, s):
            return s if sign > 0 else self.hp + s

        def key(self, sign, s):
            return self.tag + (self.index(sign, s),)

        def load_out(self, sign, s):
            link = self.axis + ("+" if sign > 0 else "-")
            return (self.key(sign, s), link, self.size / RATE, BASE + HOP)

        def send(self, sign, s):
            n = self.n
            d = lax.rem(self.pos + sign * (self.reach(sign) - s) + n, n)
            dev = self.at(lax.rem(self.pos + sign + n, n))
            m = self.index(sign, s)
            if s:
                self.copies[m - 1].wait_recv()
                ref, h = self.slot
                own, oix = self.own_ix

                def body(i, carry):
                    ref[h, m - 1, i] = ref[h, m - 1, i] + own[oix(d, i)]
                    return carry
                lax.fori_loop(0, self.lead, body, 0)
                src = ref.at[h, m - 1]
            else:
                src = self.own(d)
            ref, h = self.slot
            self.copies[m] = put(src, ref.at[h, m], self.ssem(m), self.rsem(m), dev)

        def last(self):
            return [(sign, self.reach(sign) - 1) for sign in (1, -1) if self.reach(sign)]

        def finish(self):
            ref, h = self.slot
            own, oix = self.own_ix
            last = [self.index(*e) for e in self.last()]
            for m in last:
                self.copies[m].wait_recv()

            def body(i, carry):
                total = own[oix(self.pos, i)]
                for m in last:
                    total = total + ref[h, m, i]
                own[oix(self.pos, i)] = total
                return carry
            lax.fori_loop(0, self.lead, body, 0)

        def chain(self, before, prio):
            for sign in (1, -1):
                prev = before
                for s in range(1, self.reach(sign)):
                    name = self.tag + (sign, s)
                    acts.append(Act(name, functools.partial(self.send, sign, s), after=[prev],
                                    deps=[self.key(sign, s - 1)], sends=[self.load_out(sign, s)],
                                    prio=prio))
                    prev = name

        def ends(self):
            return [self.key(*e) for e in self.last()]

    def flow(h, i):
        color, r0, nr, orient = sets[i]
        rs = pl.ds(r0, nr)
        sems = (lambda m: s1.at[h, i, m], lambda m: q1.at[h, i, m])
        sems2 = (lambda m: s2.at[h, i, m], lambda m: q2.at[h, i, m])
        t1, t2 = ("f", h, i, 1), ("f", h, i, 2)
        if color == "Y":
            first = Ring(t1, "y", ny, my_y, at_y, orient,
                         lambda d: h_ref.at[h, d, :, rs, :],
                         (h_ref, lambda d, j: (h, d, j, rs, slice(None))), nz, (slots1[i], h), *sems, nr)
            second = Ring(t2, "z", nz, my_z, at_z, orient,
                          lambda d: h_ref.at[h, my_y, pl.ds(d, 1), rs, :],
                          (h_ref, lambda d, j: (h, my_y, d, rs, slice(None))), 1, (slots2[i], h), *sems2, nr)
        else:
            first = Ring(t1, "z", nz, my_z, at_z, orient,
                         lambda d: h_ref.at[h, :, d, rs, :],
                         (h_ref, lambda d, j: (h, j, d, rs, slice(None))), ny, (slots1[i], h), *sems, nr)
            second = Ring(t2, "y", ny, my_y, at_y, orient,
                          lambda d: h_ref.at[h, pl.ds(d, 1), my_z, rs, :],
                          (h_ref, lambda d, j: (h, d, my_z, rs, slice(None))), 1, (slots2[i], h), *sems2, nr)
        prio = 10 * h
        starts = []
        for sign in (1, -1):
            if not first.reach(sign):
                continue
            if color == "Y":
                rel = (sign * first.reach(sign)) % ny
                need = [("pre", h, (ny // 2 - rel) % ny)]
            else:
                need = [("pre", h, j) for j in range(ny)]
            name = t1 + (sign, 0)
            starts.append(name)
            acts.append(Act(name, functools.partial(first.send, sign, 0), after=need,
                            sends=[first.load_out(sign, 0)], cost=0.02,
                            prio=prio + 1 - 0.1 * first.reach(sign)))
        for sign in (1, -1):
            prev = t1 + (sign, 0)
            for s in range(1, first.reach(sign)):
                name = t1 + (sign, s)
                acts.append(Act(name, functools.partial(first.send, sign, s),
                                after=[prev] + [("pre", h, j) for j in range(ny)],
                                deps=[first.key(sign, s - 1)], sends=[first.load_out(sign, s)], prio=prio))
                prev = name

        def middle():
            first.finish()
            for sign in (1, -1):
                if second.reach(sign):
                    second.send(sign, 0)
        mid = t1 + ("mid",)
        acts.append(Act(mid, middle, after=starts + [("pre", h, j) for j in range(ny)], deps=first.ends(),
                        sends=[second.load_out(sg, 0) for sg in (1, -1) if second.reach(sg)], prio=prio))
        second.chain(mid, prio)
        end = t2 + ("end",)

        def finish():
            second.finish()
            ypad[pl.ds(r0, nr), h * K:(h + 1) * K] = h_ref[h, my_y, my_z, r0:r0 + nr, :]
        acts.append(Act(end, finish, after=[mid], deps=second.ends(), prio=prio))
        return end

    def gram_sum(h, ready):
        t = ("g", h)
        off, off2 = nz + ny - 1, 2 * nz + ny - 1
        cps = {}
        piece = gz.shape[2] * K * 4

        def sem(i):
            return as_.at[h, i], ar_.at[h, i]

        def lag(j, n):
            hop = min(j, n - j)
            return BASE + HOP * hop, hop * piece / RATE

        def zlink(j):
            return "z+" if j <= nz // 2 else "z-"

        def a0():
            first_t = jnp.transpose(ypad[:, 0:K])
            gloc[h] = mm(first_t, ypad[:, h * K:(h + 1) * K]).reshape(gloc.shape[1:])
            cps["p"] = put(gloc.at[h, other], gpart.at[h], *sem(0), {"child": other})

        def a1():
            cps["p"].wait_recv()
            gz[h] = (gloc[h, c] + gpart[h]).reshape(gz.shape[1:])
            for j in zorder:
                z = lax.rem(my_z + j, nz)
                cps["z", j] = put(gz.at[h, z], zr.at[h, j - 1], *sem(j), at_z(z))

        def a2():
            total = gz[h, my_z]
            for j in zorder[::-1]:
                cps["z", j].wait_recv()
                total = total + zr[h, j - 1]
            gs[h] = total
            for j in range(1, ny):
                y = lax.rem(my_y + j, ny)
                cps["y", j] = put(gs.at[h], yr.at[h, j - 1], *sem(nz + j - 1), at_y(y))

        def a3():
            total = gs[h]
            for j in range(1, ny):
                cps["y", j].wait_recv()
                total = total + yr[h, j - 1]
            gf[h, c, my_z] = total
            for j in zorder:
                z = lax.rem(my_z + j, nz)
                cps["w", j] = put(gf.at[h, c, my_z], gf.at[h, c, my_z], *sem(off + j), at_z(z))
            cps["v", 0] = put(gf.at[h, c, my_z], gf.at[h, c, my_z], *sem(off2), {"child": other})

        def a4(j):
            cps["w", j].wait_recv()
            z = lax.rem(my_z - j + nz, nz)
            cps["v", j] = put(gf.at[h, c, z], gf.at[h, c, z], *sem(off2 + j), {"child": other})

        def a5():
            for j in range(nz):
                cps["v", j].wait_recv()

        zorder = sorted(range(1, nz), key=lambda j: -min(j, nz - j))
        acts.append(Act(t + (0,), a0, after=ready, sends=[(t + ("p",), "c", 0.3, 1.0)], cost=1.2, prio=5))
        acts.append(Act(t + (1,), a1, after=[t + (0,)], deps=[t + ("p",)], prio=5,
                        sends=[(t + ("z", j), zlink(j), lag(j, nz)[1], lag(j, nz)[0]) for j in zorder]))
        acts.append(Act(t + (2,), a2, after=[t + (1,)], deps=[t + ("z", j) for j in zorder], prio=5,
                        sends=[(t + ("y", j), "y+" if j <= ny // 2 else "y-", lag(j, ny)[1], lag(j, ny)[0])
                               for j in range(1, ny)]))
        acts.append(Act(t + (3,), a3, after=[t + (2,)], deps=[t + ("y", j) for j in range(1, ny)], prio=5,
                        sends=[(t + ("w", j), zlink(j), lag(j, nz)[1], lag(j, nz)[0]) for j in zorder]
                        + [(t + ("v", 0), "c", 0.1, 1.0)]))
        for j in range(1, nz):
            acts.append(Act(t + (4, j), functools.partial(a4, j), after=[t + (3,)], deps=[t + ("w", j)],
                            sends=[(t + ("v", j), "c", 0.1, 1.0)], cost=0.03, prio=5))
        acts.append(Act(t + (5,), a5, after=[t + (4, j) for j in range(1, nz)],
                        deps=[t + ("v", j) for j in range(nz)], cost=0.02, prio=6))
        return t + (5,)

    sub = lax.broadcasted_iota(jnp.int32, (BLK, BLK), 0)
    lane = lax.broadcasted_iota(jnp.int32, (BLK, BLK), 1)

    def chol_begin():
        aug_ref[:, 0:K] = gf[0].reshape(K, K) * scale
        big = lax.broadcasted_iota(jnp.int32, (K, K), 0) == lax.broadcasted_iota(jnp.int32, (K, K), 1)
        aug_ref[:, K:2 * K] = jnp.where(big, 1.0, 0.0)

    def chol_block(b):
        lo, hi = b * BLK, (b + 1) * BLK
        d = jnp.concatenate([aug_ref[lo:hi, lo:hi], jnp.where(sub == lane, 1.0, 0.0)], axis=1)
        for j in range(BLK):
            one = d[j:j + 1, :]
            factor = d[:, j:j + 1] * (1.0 / one[:, j:j + 1])
            factor = jnp.where(sub[:, 0:1] > j, factor, 0.0)
            d = d - factor * one
        pivots = jnp.sum(jnp.where(sub == lane, d[:, 0:BLK], 0.0), axis=1, keepdims=True)
        inv = d[:, BLK:2 * BLK] * (1.0 / jnp.sqrt(pivots))
        z = mm(inv, aug_ref[lo:hi, :])
        aug_ref[lo:hi, :] = z
        if hi < K:
            base = hi // TILE * TILE
            u = jnp.transpose(aug_ref[lo:hi, base:K])[hi - base:, :]
            aug_ref[hi:K, :] = aug_ref[hi:K, :] - mm(u, z)

    def basis():
        w = aug_ref[:, K:2 * K]
        q = lax.dot_general(ypad[:, 0:K], w, (((1,), (1,)), ((), ())), precision=HI,
                            preferred_element_type=F32)
        q_ref[...] = q[0:rows, :]
        qw_ref[...] = mm(q, w) * scale

    def fresh():
        fit = mm(qw_ref[...], gf[1].reshape(K, K))
        f_ref[...] = ypad[0:rows, K:2 * K] - fit[0:rows, :]

    for h in range(2):
        for j in range(ny):
            presum(h, j)
    ends = [[flow(h, i) for i in range(nsets)] for h in range(2)]
    g1 = gram_sum(0, ends[0])
    g2 = gram_sum(1, ends[0] + ends[1])
    acts.append(Act("chol", chol_begin, after=[g1], cost=0.3, idle=True))
    prev = "chol"
    for b in range(K // BLK):
        acts.append(Act(("chol", b), functools.partial(chol_block, b), after=[prev], cost=1.8, idle=True))
        prev = ("chol", b)
    acts.append(Act("basis", basis, after=[prev], cost=1.5, idle=True))
    acts.append(Act("fresh", fresh, after=["basis", g2], cost=1.0))
    for _, act in arrange(acts, 9.0, arrive):
        act.run()
    for h in range(2):
        for j in range(ny):
            swap(h, j).wait_send()
    for cp in pending:
        cp.wait_send()


def fused(expanded, child_map, seeds, ny, nz, rows, leaf_rows):
    sets = row_sets(rows)
    block_cols = expanded.shape[1]
    vm = pltpu.VMEM
    bf = jnp.bfloat16
    slots1 = [vm((2, (ny if s[0] == "Y" else nz) - 1, nz if s[0] == "Y" else ny, s[2], K), F32) for s in sets]
    slots2 = [vm((2, (nz if s[0] == "Y" else ny) - 1, 1, s[2], K), F32) for s in sets]
    dma = pltpu.SemaphoreType.DMA
    most = max(ny, nz) - 1
    piece = K // 2 // nz
    n_ar = 3 * nz + ny - 1
    chunk = nz * rows
    out = jax.ShapeDtypeStruct((rows, K), F32)
    return pl.pallas_call(
        functools.partial(fused_kernel, ny, nz, rows, 1.0 / leaf_rows),
        out_shape=(out, out),
        in_specs=[
            pl.BlockSpec(memory_space=pltpu.SMEM),
            pl.BlockSpec(memory_space=pltpu.VMEM),
            pl.BlockSpec(memory_space=pl.ANY),
        ],
        out_specs=[pl.BlockSpec(memory_space=pltpu.VMEM)] * 2,
        scratch_shapes=[
            *slots1, *slots2,
            vm((2 * K, block_cols), bf),
            vm((ny, chunk, block_cols), bf), vm((ny, chunk, block_cols), bf),
            vm((2, ny, nz, rows, K), F32), vm((2, ny, nz, rows, K), F32), vm((2, ny, nz, rows, K), F32),
            vm((TILE, 2 * K), F32), vm((2, 2, K // 2, K), F32), vm((2, K // 2, K), F32),
            vm((2, nz, piece, K), F32), vm((2, nz - 1, piece, K), F32), vm((2, piece, K), F32),
            vm((2, ny - 1, piece, K), F32), vm((2, 2, nz, piece, K), F32),
            vm((K, 2 * K), F32), vm((TILE, K), F32),
            dma((2, ny)), dma((2, ny)), dma((2, ny)),
            dma((2, 4, most)), dma((2, 4, most)), dma((2, 4, most)), dma((2, 4, most)),
            dma((2, n_ar)), dma((2, n_ar)),
        ],
        compiler_params=pltpu.CompilerParams(
            collective_id=0, has_side_effects=True, vmem_limit_bytes=56 << 20),
    )(seeds, child_map, expanded.reshape(2, ny, chunk, block_cols))


def make_body(parent_rows):
    def body(schur_blocks, child_map, round_seeds):
        col_count = lax.axis_size("col")
        ny, nz = GRIDS[col_count]
        leaf_rows = parent_rows // lax.axis_size("row")
        own_rows = leaf_rows // (2 * col_count)
        expanded = expand_rows(schur_blocks[0], child_map, leaf_rows)
        return fused(expanded, child_map, round_seeds, ny, nz, own_rows, leaf_rows)
    return body


def solution(mesh, parent_rows=24576):
    placed = (P("child", "row", "col"), P(), P())
    return jax.shard_map(
        make_body(parent_rows),
        mesh=mesh,
        in_specs=placed,
        out_specs=(P(("row", "child", "col"), None), P(("row", "child", "col"), None)),
        check_vma=False,
    )
```

time: 1070 us -> 125 us (0.12)
  waiting for transfers between devices: 916 us -> 0 us
  Pallas kernels: 0 us -> 116 us
  other arithmetic: 56.7 us -> 0 us
  local copies, waits for them, and re-layouts: 51 us -> 8.8 us
  matrix products: 32.8 us -> 0 us
  between operations: 16.9 us -> 0.66 us
    reduce_scatter x2 -> x0, waiting for transfers between devices: 444 us -> none  [extend(): lax.psum_scatter(partial_value, 'col', scatter_dimension=0, tiled=True)]
    psum x2 -> x0, waiting for transfers between devices: 348 us -> none  [the longest x1 175 us: body(): coefficients = lax.psum(coef_local, ('child', 'col')) / leaf_rows]
    all_gather x2 -> x0, waiting for transfers between devices: 124 us -> none  [extend(): shard_rows = lax.all_gather(summed, ('child', 'col'), axis=0, tiled=True)]
    pallas_call x0 -> x2, Pallas kernels: none -> 116 us  [the longest x1 111 us: fused(): pl.pallas_call(functools.partial(fused_kernel, ny, nz, rows, 1.0 / leaf_r...]
    another operation x10 -> x0, other arithmetic: 53.9 us -> none  [the longest x6 34.2 us: body(): lower_factor = jnp.linalg.cholesky(gram_matrix)]
    gather x1 -> x0, local copies, waits for them, and re-layouts: 45.5 us -> none  [extend(): parent_ids = jnp.take(flat_map, source)]
    dot_general x7 -> x0, matrix products: 31.7 us -> none  [the longest x2 16 us: extend(): return jnp.dot(select, shard_rows, precision=lax.Precision.HIGHEST)]
  transfers between devices with their start and end apart: 6 -> 0, of which waited for: 6 -> 0; matrix products, arithmetic and copies ran while one was open for 6% -> 0% of each run, Pallas kernels for 0% -> 0%
where the time goes in v2:
time: 125 us
  Pallas kernels  116 us (93%)
  local copies, waits for them, and re-layouts  8.8 us (7%)
    pallas_call x1, Pallas kernels, fused(): pl.pallas_call(functools.partial(fused_kernel, ny, nz, rows, 1.0 / leaf_r...  111 us
    unnamed x8, local copies, waits for them, and re-layouts  8.8 us
    pallas_call x1, Pallas kernels, expand_rows(): pl.pallas_call(expand_kernel, grid=(leaf_rows // rows,), out_shape=jax.Sh...  5.13 us

profile of v2, /device:TPU:1, one launch (start us, length us, event | category | flops | bytes accessed | tf_op | source)
XLA Modules:
  0.0 125.2 jit_solution(17918848997508310252)
XLA Ops:
  0.6 0.0 copy-start.1
  0.6 2.2 %copy-done.1 = bf16[1,4096,512]{2,1,0:T(8,128)(2,1)S(1)} copy-done((bf16[1,4096,512]{2,1,0:T(8,128)(2,1)S(1)}, bf16[1,4096,512]{2,1,0:T(8,128)(2,1)}, u32[]{:S(2)}) %copy-start.1) | copy-done | bytes 4194328
  2.8 0.0 copy-start.2
  2.8 0.9 copy-done.2
  3.7 5.1 %shard_map.50 = bf16[6144,512]{1,0:T(8,128)(2,1)S(1)} custom-call(s32[2,16384]{1,0:T(2,128)S(1)} %copy-done.2, bf16[4096,512]{1,0:T(8,128)(2,1)S(1)} %bitcast.3), custom_call_target="tpu_custom_call" | custom-call | tf_op jit(solution)/shard_map/pallas_call | solution.py:126
  8.9 0.0 copy-start
  8.9 2.6 %copy-done = bf16[6144,512]{1,0:T(8,128)(2,1)} copy-done((bf16[6144,512]{1,0:T(8,128)(2,1)}, bf16[6144,512]{1,0:T(8,128)(2,1)S(1)}, u32[]{:S(2)}) %copy-start) | copy-done | bytes 6291480
  11.5 110.6 %shard_map.51 = (f32[96,256]{1,0:T(8,128)}, f32[96,256]{1,0:T(8,128)}) custom-call(s32[2]{0:T(128)} %seeds_ref.1, s32[2,16384]{1,0:T(2,128)} %map_ref.3, bf16[2,4,768,512]{3,2,1,0:T(8,128)(2,1)} %bitcast.2), custom_call_target="tpu_custom_call" | custom-call | tf_op jit(solution)/shard_map/pallas_call | solution.py:533
  122.1 1.5 %copy.7 = f32[96,256]{1,0:T(8,128)} copy(f32[96,256]{1,0:T(8,128)} %get-tuple-element.4) | data formatting | bytes 196608
  123.7 1.5 %copy.8 = f32[96,256]{1,0:T(8,128)} copy(f32[96,256]{1,0:T(8,128)} %get-tuple-element.5) | data formatting | bytes 196608
Async XLA Ops:
  0.6 2.2 %copy-start.1 = (bf16[1,4096,512]{2,1,0:T(8,128)(2,1)S(1)}, bf16[1,4096,512]{2,1,0:T(8,128)(2,1)}, u32[]{:S(2)}) copy-start(bf16[1,4096,512]{2,1,0:T(8,128)(2,1)} %param.3) | copy-start | bytes 12582916
  2.8 0.9 copy-start.2
  8.9 2.6 %copy-start = (bf16[6144,512]{1,0:T(8,128)(2,1)}, bf16[6144,512]{1,0:T(8,128)(2,1)S(1)}, u32[]{:S(2)}) copy-start(bf16[6144,512]{1,0:T(8,128)(2,1)S(1)} %shard_map.50) | copy-start | bytes 18874372

commit v3 on v2

--- a/solution.py
+++ b/solution.py
@@ -14,8 +14,14 @@
 HI = lax.Precision.HIGHEST
 F32 = jnp.float32
 RATE = 46.0e3
-HOP = 0.75
-BASE = 1.0
+HOP = 0.8
+BASE = 1.4
+FAR = 0.15
+SETS96 = [("Y", 0, 24, 0), ("Z", 24, 16, 0), ("Y", 40, 24, 1), ("Z", 64, 16, 1), ("Y", 80, 8, 0), ("Z", 88, 8, 1)]
+
+
+def gate(i, sets):
+    return [(i, 1, 'mid')]
 
 
 def mm(a, b):
@@ -35,7 +41,7 @@
 
 def row_sets(rows):
     if rows == 96:
-        return [("Y", 0, 32, 0), ("Z", 32, 16, 0), ("Y", 48, 24, 1), ("Z", 72, 24, 1)]
+        return SETS96
     q = rows // 4
     return [("Y", 0, q, 0), ("Z", q, q, 0), ("Y", 2 * q, q, 1), ("Z", 3 * q, q, 1)]
 
@@ -46,7 +52,7 @@
 
 
 class Act:
-    def __init__(self, name, run, after=(), deps=(), sends=(), cost=0.15, idle=False, prio=0):
+    def __init__(self, name, run, after=(), deps=(), sends=(), cost=0.25, idle=False, prio=0):
         self.name, self.run, self.after, self.deps = name, run, list(after), list(deps)
         self.sends, self.cost, self.idle, self.prio = list(sends), cost, idle, prio
 
@@ -135,7 +141,7 @@
             pltpu.SMEM((8, TILE), jnp.int32),
             pltpu.SemaphoreType.DMA(()), pltpu.SemaphoreType.DMA(()),
         ],
-        compiler_params=pltpu.CompilerParams(vmem_limit_bytes=40 << 20),
+        compiler_params=pltpu.CompilerParams(vmem_limit_bytes=63 << 20),
     )(child_map, child_block)
 
 
@@ -222,22 +228,27 @@
         return carry
     lax.fori_loop(0, ny, give0, 0)
 
-    def give1(j, carry):
-        xb_ref[1, y_of(j)] = sketch(eo_ref.at[j], 1)
-        swap(1, j).start()
-        return carry
-    lax.fori_loop(0, ny, give1, 0)
-
-    def keep(j, carry):
-        y = y_of(j)
-        fetch(1, j).wait()
-        h_ref[0, y] = sketch(em_ref.at[j], 0)
-        h_ref[1, y] = sketch(em_ref.at[j], 1)
-        return carry
-    lax.fori_loop(0, ny, keep, 0)
+    def give1():
+        def body(j, carry):
+            xb_ref[1, y_of(j)] = sketch(eo_ref.at[j], 1)
+            swap(1, j).start()
+            return carry
+        lax.fori_loop(0, ny, body, 0)
+
+    def keep(h):
+        def body(j, carry):
+            if h == 0:
+                fetch(1, j).wait()
+            h_ref[h, y_of(j)] = sketch(em_ref.at[j], h)
+            return carry
+        lax.fori_loop(0, ny, body, 0)
 
     acts = []
-    arrive = {("x", h, j): 4.5 + 1.7 * (j + 1 + ny * h) for h in range(2) for j in range(ny)}
+    arrive = {("x", 0, j): 7.0 + 1.4 * j for j in range(ny)}
+    acts.append(Act("keep0", functools.partial(keep, 0), cost=2.0, prio=-2))
+    acts.append(Act("give1", give1, after=["keep0"], cost=2.0, prio=0.5,
+                    sends=[(("x", 1, j), "c", 1.4, 0.5) for j in range(ny)]))
+    acts.append(Act("keep1", functools.partial(keep, 1), after=["give1"], cost=2.0, prio=0.6))
 
     def presum(h, j):
         def run():
@@ -248,7 +259,7 @@
                 h_ref[h, y, z] = h_ref[h, y, z] + r_ref[h, y, z]
                 return carry
             lax.fori_loop(0, nz, body, 0)
-        acts.append(Act(("pre", h, j), run, deps=[("x", h, j)], cost=0.3, prio=h))
+        acts.append(Act(("pre", h, j), run, after=["keep%d" % h], deps=[("x", h, j)], cost=0.4, prio=h))
 
     class Ring:
         def __init__(self, tag, axis, n, pos, at, orient, own, own_ix, lead, slot, ssem, rsem, nr):
@@ -258,6 +269,9 @@
             self.slot, self.ssem, self.rsem = slot, ssem, rsem
             self.size = lead * nr * K * 4
             self.copies = {}
+
+        def cost(self):
+            return 0.06 + 1.6e-3 * self.size / 4096
 
         def reach(self, sign):
             return self.hp if sign > 0 else self.hm
@@ -298,7 +312,7 @@
         def finish(self):
             ref, h = self.slot
             own, oix = self.own_ix
-            last = [self.index(*e) for e in self.last()]
+            last = self.last_slots()
             for m in last:
                 self.copies[m].wait_recv()
 
@@ -317,11 +331,97 @@
                     name = self.tag + (sign, s)
                     acts.append(Act(name, functools.partial(self.send, sign, s), after=[prev],
                                     deps=[self.key(sign, s - 1)], sends=[self.load_out(sign, s)],
-                                    prio=prio))
+                                    cost=self.cost(), prio=prio))
                     prev = name
 
         def ends(self):
-            return [self.key(*e) for e in self.last()]
+            return [self.tag + (m,) for m in self.last_slots()]
+
+        def start(self):
+            for sign in (1, -1):
+                if self.reach(sign):
+                    self.send(sign, 0)
+
+        def first_sends(self):
+            return [self.load_out(sg, 0) for sg in (1, -1) if self.reach(sg)]
+
+        def more(self, before, prio):
+            self.chain(before, prio)
+            return [before]
+
+        def last_slots(self):
+            return [self.index(*e) for e in self.last()]
+
+    class Direct(Ring):
+        def start(self):
+            ref, h = self.slot
+            for j in range(1, self.n):
+                d = lax.rem(self.pos + j, self.n)
+                self.copies[j - 1] = put(self.own(d), ref.at[h, j - 1], self.ssem(j - 1), self.rsem(j - 1),
+                                         self.at(d))
+
+        def first_sends(self):
+            out = []
+            for j in range(1, self.n):
+                hop = min(j, self.n - j)
+                link = self.axis + ("+" if j <= self.n // 2 else "-")
+                out.append((self.tag + (j - 1,), link, hop * self.size / RATE, BASE + HOP + FAR * (hop - 1)))
+            return out
+
+        def more(self, before, prio):
+            return [before]
+
+        def last_slots(self):
+            return list(range(self.n - 1))
+
+    class Tree(Direct):
+        FIRST = ((0, 2, 4), (1, 1, 3), (2, 1, 1), (3, -1, -3), (4, -1, -1))
+        SECOND = ((5, 2, (0, 1)), (6, -2, (3,)))
+
+        def sign(self):
+            return 1 if self.hp >= self.hm else -1
+
+        def go(self, m, off, src):
+            ref, h = self.slot
+            dev = lax.rem(self.pos + self.sign() * off + self.n, self.n)
+            self.copies[m] = put(src, ref.at[h, m], self.ssem(m), self.rsem(m), self.at(dev))
+
+        def sim(self, m, off):
+            link = self.axis + ("+" if off * self.sign() > 0 else "-")
+            hop = abs(off)
+            return (self.tag + (m,), link, hop * self.size / RATE, BASE + HOP + FAR * (hop - 1))
+
+        def start(self):
+            for m, off, piece in self.FIRST:
+                d = lax.rem(self.pos + self.sign() * piece + self.n, self.n)
+                self.go(m, off, self.own(d))
+
+        def first_sends(self):
+            return [self.sim(m, off) for m, off, _ in self.FIRST]
+
+        def second(self, m, off, got):
+            ref, h = self.slot
+            own, oix = self.own_ix
+            d = lax.rem(self.pos + self.sign() * off + self.n, self.n)
+            total = own[oix(d, 0)]
+            for g in got:
+                self.copies[g].wait_recv()
+                total = total + ref[h, g, 0]
+            ref[h, got[0], 0] = total
+            self.go(m, off, ref.at[h, got[0]])
+
+        def more(self, before, prio):
+            names = [before]
+            for m, off, got in self.SECOND:
+                name = self.tag + ("second", m)
+                acts.append(Act(name, functools.partial(self.second, m, off, got), after=[before],
+                                deps=[self.tag + (g,) for g in got], sends=[self.sim(m, off)],
+                                cost=0.08, prio=prio))
+                names.append(name)
+            return names
+
+        def last_slots(self):
+            return [2, 4, 5, 6]
 
     def flow(h, i):
         color, r0, nr, orient = sets[i]
@@ -333,14 +433,14 @@
             first = Ring(t1, "y", ny, my_y, at_y, orient,
                          lambda d: h_ref.at[h, d, :, rs, :],
                          (h_ref, lambda d, j: (h, d, j, rs, slice(None))), nz, (slots1[i], h), *sems, nr)
-            second = Ring(t2, "z", nz, my_z, at_z, orient,
+            second = (Tree if nz == 8 else Ring)(t2, "z", nz, my_z, at_z, orient,
                           lambda d: h_ref.at[h, my_y, pl.ds(d, 1), rs, :],
                           (h_ref, lambda d, j: (h, my_y, d, rs, slice(None))), 1, (slots2[i], h), *sems2, nr)
         else:
             first = Ring(t1, "z", nz, my_z, at_z, orient,
                          lambda d: h_ref.at[h, :, d, rs, :],
                          (h_ref, lambda d, j: (h, j, d, rs, slice(None))), ny, (slots1[i], h), *sems, nr)
-            second = Ring(t2, "y", ny, my_y, at_y, orient,
+            second = Direct(t2, "y", ny, my_y, at_y, orient,
                           lambda d: h_ref.at[h, pl.ds(d, 1), my_z, rs, :],
                           (h_ref, lambda d, j: (h, d, my_z, rs, slice(None))), 1, (slots2[i], h), *sems2, nr)
         prio = 10 * h
@@ -353,10 +453,12 @@
                 need = [("pre", h, (ny // 2 - rel) % ny)]
             else:
                 need = [("pre", h, j) for j in range(ny)]
+            if h:
+                need = need + [("f", 0) + g for g in gate(i, sets)]
             name = t1 + (sign, 0)
             starts.append(name)
             acts.append(Act(name, functools.partial(first.send, sign, 0), after=need,
-                            sends=[first.load_out(sign, 0)], cost=0.02,
+                            sends=[first.load_out(sign, 0)], cost=0.03,
                             prio=prio + 1 - 0.1 * first.reach(sign)))
         for sign in (1, -1):
             prev = t1 + (sign, 0)
@@ -364,24 +466,23 @@
                 name = t1 + (sign, s)
                 acts.append(Act(name, functools.partial(first.send, sign, s),
                                 after=[prev] + [("pre", h, j) for j in range(ny)],
-                                deps=[first.key(sign, s - 1)], sends=[first.load_out(sign, s)], prio=prio))
+                                deps=[first.key(sign, s - 1)], sends=[first.load_out(sign, s)],
+                                cost=first.cost(), prio=prio))
                 prev = name
 
         def middle():
             first.finish()
-            for sign in (1, -1):
-                if second.reach(sign):
-                    second.send(sign, 0)
+            second.start()
         mid = t1 + ("mid",)
         acts.append(Act(mid, middle, after=starts + [("pre", h, j) for j in range(ny)], deps=first.ends(),
-                        sends=[second.load_out(sg, 0) for sg in (1, -1) if second.reach(sg)], prio=prio))
-        second.chain(mid, prio)
+                        sends=second.first_sends(), cost=0.06 + first.cost(), prio=prio))
+        before = second.more(mid, prio)
         end = t2 + ("end",)
 
         def finish():
             second.finish()
             ypad[pl.ds(r0, nr), h * K:(h + 1) * K] = h_ref[h, my_y, my_z, r0:r0 + nr, :]
-        acts.append(Act(end, finish, after=[mid], deps=second.ends(), prio=prio))
+        acts.append(Act(end, finish, after=before, deps=second.ends(), cost=0.1, prio=prio))
         return end
 
     def gram_sum(h, ready):
@@ -395,7 +496,7 @@
 
         def lag(j, n):
             hop = min(j, n - j)
-            return BASE + HOP * hop, hop * piece / RATE
+            return BASE + HOP + FAR * (hop - 1), hop * piece / RATE
 
         def zlink(j):
             return "z+" if j <= nz // 2 else "z-"
@@ -443,7 +544,7 @@
                 cps["v", j].wait_recv()
 
         zorder = sorted(range(1, nz), key=lambda j: -min(j, nz - j))
-        acts.append(Act(t + (0,), a0, after=ready, sends=[(t + ("p",), "c", 0.3, 1.0)], cost=1.2, prio=5))
+        acts.append(Act(t + (0,), a0, after=ready, sends=[(t + ("p",), "c", 0.3, 1.0)], cost=1.8, prio=5))
         acts.append(Act(t + (1,), a1, after=[t + (0,)], deps=[t + ("p",)], prio=5,
                         sends=[(t + ("z", j), zlink(j), lag(j, nz)[1], lag(j, nz)[0]) for j in zorder]))
         acts.append(Act(t + (2,), a2, after=[t + (1,)], deps=[t + ("z", j) for j in zorder], prio=5,
@@ -469,20 +570,45 @@
 
     def chol_block(b):
         lo, hi = b * BLK, (b + 1) * BLK
-        d = jnp.concatenate([aug_ref[lo:hi, lo:hi], jnp.where(sub == lane, 1.0, 0.0)], axis=1)
-        for j in range(BLK):
-            one = d[j:j + 1, :]
-            factor = d[:, j:j + 1] * (1.0 / one[:, j:j + 1])
-            factor = jnp.where(sub[:, 0:1] > j, factor, 0.0)
-            d = d - factor * one
-        pivots = jnp.sum(jnp.where(sub == lane, d[:, 0:BLK], 0.0), axis=1, keepdims=True)
-        inv = d[:, BLK:2 * BLK] * (1.0 / jnp.sqrt(pivots))
-        z = mm(inv, aug_ref[lo:hi, :])
-        aug_ref[lo:hi, :] = z
+        both = jnp.concatenate([aug_ref[lo:hi, lo:hi], jnp.where(sub == lane, 1.0, 0.0)], axis=1)
+        d = [both[8 * g:8 * g + 8, :] for g in range(BLK // 8)]
+        sub8 = lax.broadcasted_iota(jnp.int32, (8, 2 * BLK), 0)
+        lane8 = lax.broadcasted_iota(jnp.int32, (8, 2 * BLK), 1)
+        for p in range(0, BLK, 2):
+            g0, q = p // 8, p % 8
+            row0, row1 = d[g0][q:q + 1, :], d[g0][q + 1:q + 2, :]
+            col0 = [jnp.broadcast_to(x[:, p:p + 1], x.shape) for x in d[g0:]]
+            col1 = [jnp.broadcast_to(x[:, p + 1:p + 2], x.shape) for x in d[g0:]]
+            aa, ab, bb = col0[0][q:q + 1, :], col0[0][q + 1:q + 2, :], col1[0][q + 1:q + 2, :]
+            inv_det = 1.0 / (aa * bb - ab * ab)
+            mix0 = (bb * inv_det) * row0 - (ab * inv_det) * row1
+            mix1 = (aa * inv_det) * row1 - (ab * inv_det) * row0
+            for g in range(g0, BLK // 8):
+                x0, x1 = col0[g - g0], col1[g - g0]
+                if g == g0:
+                    if q == 6:
+                        continue
+                    x0 = jnp.where(sub8 > q + 1, x0, 0.0)
+                    x1 = jnp.where(sub8 > q + 1, x1, 0.0)
+                d[g] = d[g] - (x0 * mix0 + x1 * mix1)
+        out = []
+        for g in range(BLK // 8):
+            me = sub8 + 8 * g
+            diag = jnp.sum(jnp.where(lane8 == me, d[g], 0.0), axis=1, keepdims=True)
+            side = jnp.where((lane8 == me - 1) & (sub8 % 2 == 1), d[g], 0.0)
+            side = jnp.sum(side, axis=1, keepdims=True)
+            wide = jnp.broadcast_to(diag, d[g].shape)
+            lift = side / pltpu.roll(wide, 1, 0)
+            full = d[g] - lift * pltpu.roll(d[g], 1, 0)
+            out.append(full * (1.0 / jnp.sqrt(wide - lift * side)))
+        inv = jnp.concatenate(out, axis=0)[:, BLK:2 * BLK]
+        left, right = (0, K + TILE) if hi <= TILE else (TILE, 2 * K)
+        z = mm(inv, aug_ref[lo:hi, left:right])
+        aug_ref[lo:hi, left:right] = z
         if hi < K:
             base = hi // TILE * TILE
             u = jnp.transpose(aug_ref[lo:hi, base:K])[hi - base:, :]
-            aug_ref[hi:K, :] = aug_ref[hi:K, :] - mm(u, z)
+            aug_ref[hi:K, left:right] = aug_ref[hi:K, left:right] - mm(u, z)
 
     def basis():
         w = aug_ref[:, K:2 * K]
@@ -504,11 +630,11 @@
     acts.append(Act("chol", chol_begin, after=[g1], cost=0.3, idle=True))
     prev = "chol"
     for b in range(K // BLK):
-        acts.append(Act(("chol", b), functools.partial(chol_block, b), after=[prev], cost=1.8, idle=True))
+        acts.append(Act(("chol", b), functools.partial(chol_block, b), after=[prev], cost=1.4, idle=True))
         prev = ("chol", b)
-    acts.append(Act("basis", basis, after=[prev], cost=1.5, idle=True))
-    acts.append(Act("fresh", fresh, after=["basis", g2], cost=1.0))
-    for _, act in arrange(acts, 9.0, arrive):
+    acts.append(Act("basis", basis, after=[prev], cost=2.0, idle=True))
+    acts.append(Act("fresh", fresh, after=["basis", g2], cost=1.2))
+    for _, act in arrange(acts, 7.0, arrive):
         act.run()
     for h in range(2):
         for j in range(ny):
@@ -522,8 +648,8 @@
     block_cols = expanded.shape[1]
     vm = pltpu.VMEM
     bf = jnp.bfloat16
-    slots1 = [vm((2, (ny if s[0] == "Y" else nz) - 1, nz if s[0] == "Y" else ny, s[2], K), F32) for s in sets]
-    slots2 = [vm((2, (nz if s[0] == "Y" else ny) - 1, 1, s[2], K), F32) for s in sets]
+    slots1 = [vm((2, max(1, (ny if s[0] == "Y" else nz) - 1), nz if s[0] == "Y" else ny, s[2], K), F32) for s in sets]
+    slots2 = [vm((2, max(1, (nz if s[0] == "Y" else ny) - 1), 1, s[2], K), F32) for s in sets]
     dma = pltpu.SemaphoreType.DMA
     most = max(ny, nz) - 1
     piece = K // 2 // nz
@@ -546,14 +672,14 @@
             vm((2, ny, nz, rows, K), F32), vm((2, ny, nz, rows, K), F32), vm((2, ny, nz, rows, K), F32),
             vm((TILE, 2 * K), F32), vm((2, 2, K // 2, K), F32), vm((2, K // 2, K), F32),
             vm((2, nz, piece, K), F32), vm((2, nz - 1, piece, K), F32), vm((2, piece, K), F32),
-            vm((2, ny - 1, piece, K), F32), vm((2, 2, nz, piece, K), F32),
+            vm((2, max(1, ny - 1), piece, K), F32), vm((2, 2, nz, piece, K), F32),
             vm((K, 2 * K), F32), vm((TILE, K), F32),
             dma((2, ny)), dma((2, ny)), dma((2, ny)),
-            dma((2, 4, most)), dma((2, 4, most)), dma((2, 4, most)), dma((2, 4, most)),
+            *[dma((2, len(sets), most))] * 4,
             dma((2, n_ar)), dma((2, n_ar)),
         ],
         compiler_params=pltpu.CompilerParams(
-            collective_id=0, has_side_effects=True, vmem_limit_bytes=56 << 20),
+            collective_id=0, has_side_effects=True, vmem_limit_bytes=63 << 20),
     )(seeds, child_map, expanded.reshape(2, ny, chunk, block_cols))
 
 

time: 125 us -> 118 us (0.944)
  local copies, waits for them, and re-layouts: 8.8 us -> 3.08 us
  Pallas kernels: 116 us -> 114 us
    pallas_call x1, Pallas kernels: 111 us -> 104 us  [fused(): pl.pallas_call(functools.partial(fused_kernel, ny, nz, rows, 1.0 / leaf_r...]
    unnamed x8 -> x2, local copies, waits for them, and re-layouts: 8.8 us -> 3.08 us
    pallas_call x1, Pallas kernels: 5.13 us -> 10.2 us  [expand_rows(): pl.pallas_call(expand_kernel, grid=(leaf_rows // rows,), out_shape=jax.Sh...]
where the time goes in v3:
time: 118 us
  Pallas kernels  114 us (97%)
  local copies, waits for them, and re-layouts  3.08 us (3%)
    pallas_call x1, Pallas kernels, fused(): pl.pallas_call(functools.partial(fused_kernel, ny, nz, rows, 1.0 / leaf_r...  104 us
    pallas_call x1, Pallas kernels, expand_rows(): pl.pallas_call(expand_kernel, grid=(leaf_rows // rows,), out_shape=jax.Sh...  10.2 us
    unnamed x2, local copies, waits for them, and re-layouts  3.08 us

profile of v3, /device:TPU:1, one launch (start us, length us, event | category | flops | bytes accessed | tf_op | source)
XLA Modules:
  0.0 118.2 jit_solution(2500719196916960840)
XLA Ops:
  0.6 10.2 %shard_map.50 = bf16[6144,512]{1,0:T(8,128)(2,1)} custom-call(s32[2,16384]{1,0:T(2,128)} %map_ref.3, bf16[4096,512]{1,0:T(8,128)(2,1)} %bitcast.3), custom_call_target="tpu_custom_call" | custom-call | tf_op jit(solution)/shard_map/pallas_call | solution.py:132
  10.8 104.3 %shard_map.51 = (f32[96,256]{1,0:T(8,128)}, f32[96,256]{1,0:T(8,128)}) custom-call(s32[2]{0:T(128)} %seeds_ref.1, s32[2,16384]{1,0:T(2,128)} %map_ref.3, bf16[2,4,768,512]{3,2,1,0:T(8,128)(2,1)} %bitcast.2), custom_call_target="tpu_custom_call" | custom-call | tf_op jit(solution)/shard_map/pallas_call | solution.py:659
  115.1 1.5 %copy.7 = f32[96,256]{1,0:T(8,128)} copy(f32[96,256]{1,0:T(8,128)} %get-tuple-element.4) | data formatting | bytes 196608
  116.7 1.5 %copy.8 = f32[96,256]{1,0:T(8,128)} copy(f32[96,256]{1,0:T(8,128)} %get-tuple-element.5) | data formatting | bytes 196608

commit v4 on v3

--- a/solution.py
+++ b/solution.py
@@ -8,10 +8,9 @@
 
 K = 256
 TILE = 128
-BLK = 32
+BLK = 64
 GRIDS = {32: (4, 8), 8: (2, 4)}
 MESH = pl.DeviceIdType.MESH
-HI = lax.Precision.HIGHEST
 F32 = jnp.float32
 RATE = 46.0e3
 HOP = 0.8
@@ -24,8 +23,17 @@
     return [(i, 1, 'mid')]
 
 
-def mm(a, b):
-    return jnp.dot(a, b, precision=HI, preferred_element_type=F32)
+def split(x):
+    high = x.astype(jnp.bfloat16)
+    return high, (x - high.astype(F32)).astype(jnp.bfloat16)
+
+
+def mm(a, b, dims=(((1,), (0,)), ((), ()))):
+    (ah, al), (bh, bl) = split(a), split(b)
+
+    def dot(x, y):
+        return lax.dot_general(x, y, dims, preferred_element_type=F32)
+    return dot(ah, bh) + (dot(ah, bl) + dot(al, bh))
 
 
 def hash_values(ids_row, col, seed):
@@ -141,7 +149,7 @@
             pltpu.SMEM((8, TILE), jnp.int32),
             pltpu.SemaphoreType.DMA(()), pltpu.SemaphoreType.DMA(()),
         ],
-        compiler_params=pltpu.CompilerParams(vmem_limit_bytes=63 << 20),
+        compiler_params=pltpu.CompilerParams(vmem_limit_bytes=40 << 20),
     )(child_map, child_block)
 
 
@@ -149,9 +157,10 @@
     sets = row_sets(rows)
     nsets = len(sets)
     slots1, slots2 = refs[:nsets], refs[nsets:2 * nsets]
+    got1, got2 = refs[2 * nsets:3 * nsets], refs[3 * nsets:4 * nsets]
     (st_ref, eo_ref, em_ref, xb_ref, h_ref, r_ref,
      ypad, gloc, gpart, gz, zr, gs, yr, gf, aug_ref, qw_ref,
-     e_sem, xs, xr, s1, q1, s2, q2, as_, ar_) = refs[2 * nsets:]
+     e_sem, xs, xr, s1, s2, as_, ar_) = refs[4 * nsets:]
 
     block_cols = em_ref.shape[2]
 
@@ -167,7 +176,7 @@
     def at_z(z):
         return {"col": my_y * nz + z}
 
-    pending = []
+    sent = []
 
     def remote(src, dst, ssem, rsem, dev):
         return pltpu.make_async_remote_copy(
@@ -177,7 +186,6 @@
     def put(*args):
         cp = remote(*args)
         cp.start()
-        pending.append(cp)
         return cp
 
     def y_of(j):
@@ -185,7 +193,7 @@
 
     def fetch(side, j):
         half, dst = ((other, eo_ref), (c, em_ref))[side]
-        return pltpu.make_async_copy(e_hbm.at[half, y_of(j)], dst.at[j], e_sem.at[side, j])
+        return pltpu.make_async_copy(e_hbm.at[half, y_of(j)], dst.at[j], e_sem.at[ny if side else j])
 
     for side in range(2):
         for j in range(ny):
@@ -216,7 +224,7 @@
 
     def swap(h, j):
         y = y_of(j)
-        return remote(xb_ref.at[h, y], r_ref.at[h, y], xs.at[h, j], xr.at[h, j], {"child": other})
+        return remote(xb_ref.at[h, y], r_ref.at[h, y], xs.at[0], xr.at[h, j], {"child": other})
 
     pl.semaphore_wait(barrier, len(peers))
 
@@ -236,9 +244,10 @@
         lax.fori_loop(0, ny, body, 0)
 
     def keep(h):
+        if h == 0:
+            pltpu.make_async_copy(em_ref, em_ref, e_sem.at[ny]).wait()
+
         def body(j, carry):
-            if h == 0:
-                fetch(1, j).wait()
             h_ref[h, y_of(j)] = sketch(em_ref.at[j], h)
             return carry
         lax.fori_loop(0, ny, body, 0)
@@ -268,7 +277,23 @@
             self.own, self.own_ix, self.lead = own, own_ix, lead
             self.slot, self.ssem, self.rsem = slot, ssem, rsem
             self.size = lead * nr * K * 4
-            self.copies = {}
+            self.groups = self.group()
+
+        def group(self):
+            last = self.last_slots()
+            return [last] + [[m] for m in range(self.n - 1) if m not in last]
+
+        def sem_of(self, m):
+            return self.rsem([m in g for g in self.groups].index(True))
+
+        def wait(self, which):
+            ref, h = self.slot
+            if self.groups[which]:
+                span = ref.at[h, pl.ds(0, len(self.groups[which]))]
+                remote(span, span, self.ssem, self.rsem(which), {"child": other}).wait_recv()
+
+        def wait_for(self, m):
+            self.wait([m in g for g in self.groups].index(True))
 
         def cost(self):
             return 0.06 + 1.6e-3 * self.size / 4096
@@ -292,7 +317,7 @@
             dev = self.at(lax.rem(self.pos + sign + n, n))
             m = self.index(sign, s)
             if s:
-                self.copies[m - 1].wait_recv()
+                self.wait_for(m - 1)
                 ref, h = self.slot
                 own, oix = self.own_ix
 
@@ -304,7 +329,7 @@
             else:
                 src = self.own(d)
             ref, h = self.slot
-            self.copies[m] = put(src, ref.at[h, m], self.ssem(m), self.rsem(m), dev)
+            put(src, ref.at[h, m], self.ssem, self.sem_of(m), dev)
 
         def last(self):
             return [(sign, self.reach(sign) - 1) for sign in (1, -1) if self.reach(sign)]
@@ -313,8 +338,7 @@
             ref, h = self.slot
             own, oix = self.own_ix
             last = self.last_slots()
-            for m in last:
-                self.copies[m].wait_recv()
+            self.wait(0)
 
             def body(i, carry):
                 total = own[oix(self.pos, i)]
@@ -357,8 +381,7 @@
             ref, h = self.slot
             for j in range(1, self.n):
                 d = lax.rem(self.pos + j, self.n)
-                self.copies[j - 1] = put(self.own(d), ref.at[h, j - 1], self.ssem(j - 1), self.rsem(j - 1),
-                                         self.at(d))
+                put(self.own(d), ref.at[h, j - 1], self.ssem, self.sem_of(j - 1), self.at(d))
 
         def first_sends(self):
             out = []
@@ -384,7 +407,7 @@
         def go(self, m, off, src):
             ref, h = self.slot
             dev = lax.rem(self.pos + self.sign() * off + self.n, self.n)
-            self.copies[m] = put(src, ref.at[h, m], self.ssem(m), self.rsem(m), self.at(dev))
+            put(src, ref.at[h, m], self.ssem, self.sem_of(m), self.at(dev))
 
         def sim(self, m, off):
             link = self.axis + ("+" if off * self.sign() > 0 else "-")
@@ -404,8 +427,8 @@
             own, oix = self.own_ix
             d = lax.rem(self.pos + self.sign() * off + self.n, self.n)
             total = own[oix(d, 0)]
+            self.wait_for(got[0])
             for g in got:
-                self.copies[g].wait_recv()
                 total = total + ref[h, g, 0]
             ref[h, got[0], 0] = total
             self.go(m, off, ref.at[h, got[0]])
@@ -423,11 +446,14 @@
         def last_slots(self):
             return [2, 4, 5, 6]
 
+        def group(self):
+            return [self.last_slots(), [0, 1], [3]]
+
     def flow(h, i):
         color, r0, nr, orient = sets[i]
         rs = pl.ds(r0, nr)
-        sems = (lambda m: s1.at[h, i, m], lambda m: q1.at[h, i, m])
-        sems2 = (lambda m: s2.at[h, i, m], lambda m: q2.at[h, i, m])
+        sems = (s1.at[i], lambda m: got1[i].at[h, m])
+        sems2 = (s2.at[i], lambda m: got2[i].at[h, m])
         t1, t2 = ("f", h, i, 1), ("f", h, i, 2)
         if color == "Y":
             first = Ring(t1, "y", ny, my_y, at_y, orient,
@@ -443,6 +469,8 @@
             second = Direct(t2, "y", ny, my_y, at_y, orient,
                           lambda d: h_ref.at[h, pl.ds(d, 1), my_z, rs, :],
                           (h_ref, lambda d, j: (h, d, my_z, rs, slice(None))), 1, (slots2[i], h), *sems2, nr)
+        if h:
+            sent.extend((ring.ssem, buf) for ring, buf in ((first, slots1[i]), (second, slots2[i])) if ring.n > 1)
         prio = 10 * h
         starts = []
         for sign in (1, -1):
@@ -487,12 +515,18 @@
 
     def gram_sum(h, ready):
         t = ("g", h)
-        off, off2 = nz + ny - 1, 2 * nz + ny - 1
-        cps = {}
         piece = gz.shape[2] * K * 4
 
         def sem(i):
             return as_.at[h, i], ar_.at[h, i]
+
+        def wait(i, buf):
+            remote(buf, buf, *sem(i), {"child": other}).wait_recv()
+
+        def total_of(start, parts, count):
+            for j in range(count):
+                start = start + parts[h, j]
+            return start
 
         def lag(j, n):
             hop = min(j, n - j)
@@ -504,60 +538,54 @@
         def a0():
             first_t = jnp.transpose(ypad[:, 0:K])
             gloc[h] = mm(first_t, ypad[:, h * K:(h + 1) * K]).reshape(gloc.shape[1:])
-            cps["p"] = put(gloc.at[h, other], gpart.at[h], *sem(0), {"child": other})
+            put(gloc.at[h, other], gpart.at[h], *sem(0), {"child": other})
 
         def a1():
-            cps["p"].wait_recv()
+            wait(0, gpart.at[h])
             gz[h] = (gloc[h, c] + gpart[h]).reshape(gz.shape[1:])
             for j in zorder:
                 z = lax.rem(my_z + j, nz)
-                cps["z", j] = put(gz.at[h, z], zr.at[h, j - 1], *sem(j), at_z(z))
+                put(gz.at[h, z], zr.at[h, j - 1], *sem(1), at_z(z))
 
         def a2():
-            total = gz[h, my_z]
-            for j in zorder[::-1]:
-                cps["z", j].wait_recv()
-                total = total + zr[h, j - 1]
+            wait(1, zr.at[h])
+            total = total_of(gz[h, my_z], zr, nz - 1)
             gs[h] = total
             for j in range(1, ny):
                 y = lax.rem(my_y + j, ny)
-                cps["y", j] = put(gs.at[h], yr.at[h, j - 1], *sem(nz + j - 1), at_y(y))
+                put(gs.at[h], yr.at[h, j - 1], *sem(2), at_y(y))
 
         def a3():
-            total = gs[h]
-            for j in range(1, ny):
-                cps["y", j].wait_recv()
-                total = total + yr[h, j - 1]
+            if ny > 1:
+                wait(2, yr.at[h])
+            total = total_of(gs[h], yr, ny - 1)
             gf[h, c, my_z] = total
             for j in zorder:
                 z = lax.rem(my_z + j, nz)
-                cps["w", j] = put(gf.at[h, c, my_z], gf.at[h, c, my_z], *sem(off + j), at_z(z))
-            cps["v", 0] = put(gf.at[h, c, my_z], gf.at[h, c, my_z], *sem(off2), {"child": other})
-
-        def a4(j):
-            cps["w", j].wait_recv()
-            z = lax.rem(my_z - j + nz, nz)
-            cps["v", j] = put(gf.at[h, c, z], gf.at[h, c, z], *sem(off2 + j), {"child": other})
+                put(gf.at[h, c, my_z], gf.at[h, c, my_z], *sem(3), at_z(z))
+
+        def a4():
+            wait(3, zr.at[h])
+            put(gf.at[h, c], gf.at[h, c], *sem(4), {"child": other})
 
         def a5():
-            for j in range(nz):
-                cps["v", j].wait_recv()
-
+            wait(4, gf.at[h, c])
+
+        for i, buf in enumerate((gpart, zr, yr, zr, gpart)):
+            if i != 2 or ny > 1:
+                sent.append((as_.at[h, i], buf.at[h]))
         zorder = sorted(range(1, nz), key=lambda j: -min(j, nz - j))
-        acts.append(Act(t + (0,), a0, after=ready, sends=[(t + ("p",), "c", 0.3, 1.0)], cost=1.8, prio=5))
+        acts.append(Act(t + (0,), a0, after=ready, sends=[(t + ("p",), "c", 0.3, 1.0)], cost=1.2, prio=5))
         acts.append(Act(t + (1,), a1, after=[t + (0,)], deps=[t + ("p",)], prio=5,
                         sends=[(t + ("z", j), zlink(j), lag(j, nz)[1], lag(j, nz)[0]) for j in zorder]))
         acts.append(Act(t + (2,), a2, after=[t + (1,)], deps=[t + ("z", j) for j in zorder], prio=5,
                         sends=[(t + ("y", j), "y+" if j <= ny // 2 else "y-", lag(j, ny)[1], lag(j, ny)[0])
                                for j in range(1, ny)]))
         acts.append(Act(t + (3,), a3, after=[t + (2,)], deps=[t + ("y", j) for j in range(1, ny)], prio=5,
-                        sends=[(t + ("w", j), zlink(j), lag(j, nz)[1], lag(j, nz)[0]) for j in zorder]
-                        + [(t + ("v", 0), "c", 0.1, 1.0)]))
-        for j in range(1, nz):
-            acts.append(Act(t + (4, j), functools.partial(a4, j), after=[t + (3,)], deps=[t + ("w", j)],
-                            sends=[(t + ("v", j), "c", 0.1, 1.0)], cost=0.03, prio=5))
-        acts.append(Act(t + (5,), a5, after=[t + (4, j) for j in range(1, nz)],
-                        deps=[t + ("v", j) for j in range(nz)], cost=0.02, prio=6))
+                        sends=[(t + ("w", j), zlink(j), lag(j, nz)[1], lag(j, nz)[0]) for j in zorder]))
+        acts.append(Act(t + (4,), a4, after=[t + (3,)], deps=[t + ("w", j) for j in zorder],
+                        sends=[(t + ("v",), "c", 0.3, 1.0)], cost=0.05, prio=5))
+        acts.append(Act(t + (5,), a5, after=[t + (4,)], deps=[t + ("v",)], cost=0.02, prio=6))
         return t + (5,)
 
     sub = lax.broadcasted_iota(jnp.int32, (BLK, BLK), 0)
@@ -612,8 +640,7 @@
 
     def basis():
         w = aug_ref[:, K:2 * K]
-        q = lax.dot_general(ypad[:, 0:K], w, (((1,), (1,)), ((), ())), precision=HI,
-                            preferred_element_type=F32)
+        q = mm(ypad[:, 0:K], w, (((1,), (1,)), ((), ())))
         q_ref[...] = q[0:rows, :]
         qw_ref[...] = mm(q, w) * scale
 
@@ -630,17 +657,15 @@
     acts.append(Act("chol", chol_begin, after=[g1], cost=0.3, idle=True))
     prev = "chol"
     for b in range(K // BLK):
-        acts.append(Act(("chol", b), functools.partial(chol_block, b), after=[prev], cost=1.4, idle=True))
+        acts.append(Act(("chol", b), functools.partial(chol_block, b), after=[prev], cost=3.3, idle=True))
         prev = ("chol", b)
     acts.append(Act("basis", basis, after=[prev], cost=2.0, idle=True))
     acts.append(Act("fresh", fresh, after=["basis", g2], cost=1.2))
     for _, act in arrange(acts, 7.0, arrive):
         act.run()
-    for h in range(2):
-        for j in range(ny):
-            swap(h, j).wait_send()
-    for cp in pending:
-        cp.wait_send()
+    sent.append((xs.at[0], xb_ref))
+    for sem, buf in sent:
+        remote(buf, buf, sem, sem, {"child": other}).wait_send()
 
 
 def fused(expanded, child_map, seeds, ny, nz, rows, leaf_rows):
@@ -651,9 +676,11 @@
     slots1 = [vm((2, max(1, (ny if s[0] == "Y" else nz) - 1), nz if s[0] == "Y" else ny, s[2], K), F32) for s in sets]
     slots2 = [vm((2, max(1, (nz if s[0] == "Y" else ny) - 1), 1, s[2], K), F32) for s in sets]
     dma = pltpu.SemaphoreType.DMA
-    most = max(ny, nz) - 1
+
+    def groups(n):
+        return max(1, n - 1 - sum(1 for r in hops(n, 0) if r) + 1)
+
     piece = K // 2 // nz
-    n_ar = 3 * nz + ny - 1
     chunk = nz * rows
     out = jax.ShapeDtypeStruct((rows, K), F32)
     return pl.pallas_call(
@@ -667,6 +694,8 @@
         out_specs=[pl.BlockSpec(memory_space=pltpu.VMEM)] * 2,
         scratch_shapes=[
             *slots1, *slots2,
+            *[dma((2, groups(ny if s[0] == "Y" else nz))) for s in sets],
+            *[dma((2, 3 if s[0] == "Y" and nz == 8 else groups(nz) if s[0] == "Y" else 1)) for s in sets],
             vm((2 * K, block_cols), bf),
             vm((ny, chunk, block_cols), bf), vm((ny, chunk, block_cols), bf),
             vm((2, ny, nz, rows, K), F32), vm((2, ny, nz, rows, K), F32), vm((2, ny, nz, rows, K), F32),
@@ -674,9 +703,8 @@
             vm((2, nz, piece, K), F32), vm((2, nz - 1, piece, K), F32), vm((2, piece, K), F32),
             vm((2, max(1, ny - 1), piece, K), F32), vm((2, 2, nz, piece, K), F32),
             vm((K, 2 * K), F32), vm((TILE, K), F32),
-            dma((2, ny)), dma((2, ny)), dma((2, ny)),
-            *[dma((2, len(sets), most))] * 4,
-            dma((2, n_ar)), dma((2, n_ar)),
+            dma((ny + 1,)), dma((1,)), dma((2, ny)),
+            dma((len(sets),)), dma((len(sets),)), dma((2, 5)), dma((2, 5)),
         ],
         compiler_params=pltpu.CompilerParams(
             collective_id=0, has_side_effects=True, vmem_limit_bytes=63 << 20),

time: 118 us -> 112 us (0.949)
  Pallas kernels: 114 us -> 102 us
  local copies, waits for them, and re-layouts: 3.08 us -> 8.8 us
    pallas_call x1, Pallas kernels: 104 us -> 96.8 us  [fused(): pl.pallas_call(functools.partial(fused_kernel, ny, nz, rows, 1.0 / leaf_r...]
    unnamed x2 -> x8, local copies, waits for them, and re-layouts: 3.08 us -> 8.8 us
    pallas_call x1, Pallas kernels: 10.2 us -> 5.13 us  [expand_rows(): pl.pallas_call(expand_kernel, grid=(leaf_rows // rows,), out_shape=jax.Sh...]
where the time goes in v4:
time: 112 us; the launch traced here: 111 us
  Pallas kernels  102 us (91%)
  local copies, waits for them, and re-layouts  8.8 us (8%)
    pallas_call x1, Pallas kernels, fused(): pl.pallas_call(functools.partial(fused_kernel, ny, nz, rows, 1.0 / leaf_r...  96.8 us
    unnamed x8, local copies, waits for them, and re-layouts  8.8 us
    pallas_call x1, Pallas kernels, expand_rows(): pl.pallas_call(expand_kernel, grid=(leaf_rows // rows,), out_shape=jax.Sh...  5.13 us

profile of v4, /device:TPU:1, one launch (start us, length us, event | category | flops | bytes accessed | tf_op | source)
XLA Modules:
  0.0 111.4 jit_solution(6791641329993155577)
XLA Ops:
  0.6 0.0 copy-start.1
  0.6 2.2 %copy-done.1 = bf16[1,4096,512]{2,1,0:T(8,128)(2,1)S(1)} copy-done((bf16[1,4096,512]{2,1,0:T(8,128)(2,1)S(1)}, bf16[1,4096,512]{2,1,0:T(8,128)(2,1)}, u32[]{:S(2)}) %copy-start.1) | copy-done | bytes 4194328
  2.8 0.0 copy-start.2
  2.8 0.9 copy-done.2
  3.7 5.1 %shard_map.50 = bf16[6144,512]{1,0:T(8,128)(2,1)S(1)} custom-call(s32[2,16384]{1,0:T(2,128)S(1)} %copy-done.2, bf16[4096,512]{1,0:T(8,128)(2,1)S(1)} %bitcast.3), custom_call_target="tpu_custom_call" | custom-call | tf_op jit(solution)/shard_map/pallas_call | solution.py:140
  8.9 0.0 copy-start
  8.9 2.6 %copy-done = bf16[6144,512]{1,0:T(8,128)(2,1)} copy-done((bf16[6144,512]{1,0:T(8,128)(2,1)}, bf16[6144,512]{1,0:T(8,128)(2,1)S(1)}, u32[]{:S(2)}) %copy-start) | copy-done | bytes 6291480
  11.5 96.8 %shard_map.51 = (f32[96,256]{1,0:T(8,128)}, f32[96,256]{1,0:T(8,128)}) custom-call(s32[2]{0:T(128)} %seeds_ref.1, s32[2,16384]{1,0:T(2,128)} %map_ref.3, bf16[2,4,768,512]{3,2,1,0:T(8,128)(2,1)} %bitcast.2), custom_call_target="tpu_custom_call" | custom-call | tf_op jit(solution)/shard_map/pallas_call | solution.py:686
  108.3 1.5 %copy.7 = f32[96,256]{1,0:T(8,128)} copy(f32[96,256]{1,0:T(8,128)} %get-tuple-element.4) | data formatting | bytes 196608
  109.8 1.5 %copy.8 = f32[96,256]{1,0:T(8,128)} copy(f32[96,256]{1,0:T(8,128)} %get-tuple-element.5) | data formatting | bytes 196608
Async XLA Ops:
  0.6 2.2 %copy-start.1 = (bf16[1,4096,512]{2,1,0:T(8,128)(2,1)S(1)}, bf16[1,4096,512]{2,1,0:T(8,128)(2,1)}, u32[]{:S(2)}) copy-start(bf16[1,4096,512]{2,1,0:T(8,128)(2,1)} %param.3) | copy-start | bytes 12582916
  2.8 0.9 copy-start.2
  8.9 2.6 %copy-start = (bf16[6144,512]{1,0:T(8,128)(2,1)}, bf16[6144,512]{1,0:T(8,128)(2,1)S(1)}, u32[]{:S(2)}) copy-start(bf16[6144,512]{1,0:T(8,128)(2,1)S(1)} %shard_map.50) | copy-start | bytes 18874372

commit v5 on v4

--- a/solution.py
+++ b/solution.py
@@ -16,11 +16,12 @@
 HOP = 0.8
 BASE = 1.4
 FAR = 0.15
-SETS96 = [("Y", 0, 24, 0), ("Z", 24, 16, 0), ("Y", 40, 24, 1), ("Z", 64, 16, 1), ("Y", 80, 8, 0), ("Z", 88, 8, 1)]
+SETS96 = [("Z", 0, 16, 1), ("Y", 16, 8, 1), ("Y", 24, 8, 0), ("Y", 32, 24, 1), ("Z", 56, 8, 1), ("Z", 64, 16, 0), ("Y", 80, 16, 0)]
+GATES96 = [[(0, 1, "mid")], [(0, 2, "end")], [(2, 1, "mid")], [(3, 1, "mid")], [(2, 2, "end")], [(5, 1, "mid")], [(5, 2, "end")]]
 
 
 def gate(i, sets):
-    return [(i, 1, 'mid')]
+    return GATES96[i] if sets == SETS96 else [(i, 1, 'mid')]
 
 
 def split(x):
@@ -149,17 +150,17 @@
             pltpu.SMEM((8, TILE), jnp.int32),
             pltpu.SemaphoreType.DMA(()), pltpu.SemaphoreType.DMA(()),
         ],
-        compiler_params=pltpu.CompilerParams(vmem_limit_bytes=40 << 20),
+        compiler_params=pltpu.CompilerParams(vmem_limit_bytes=48 << 20),
     )(child_map, child_block)
 
 
-def fused_kernel(ny, nz, rows, scale, seeds_ref, map_ref, e_hbm, q_ref, f_ref, *refs):
+def fused_kernel(ny, nz, rows, scale, seeds_ref, map_ref, e_hbm, q_ref, y2_ref, qw_ref, g_ref, *refs):
     sets = row_sets(rows)
     nsets = len(sets)
     slots1, slots2 = refs[:nsets], refs[nsets:2 * nsets]
     got1, got2 = refs[2 * nsets:3 * nsets], refs[3 * nsets:4 * nsets]
     (st_ref, eo_ref, em_ref, xb_ref, h_ref, r_ref,
-     ypad, gloc, gpart, gz, zr, gs, yr, gf, aug_ref, qw_ref,
+     ypad, gloc, gpart, gz, zr, gs, yr, gf, aug_ref,
      e_sem, xs, xr, s1, s2, as_, ar_) = refs[4 * nsets:]
 
     block_cols = em_ref.shape[2]
@@ -642,11 +643,11 @@
         w = aug_ref[:, K:2 * K]
         q = mm(ypad[:, 0:K], w, (((1,), (1,)), ((), ())))
         q_ref[...] = q[0:rows, :]
-        qw_ref[...] = mm(q, w) * scale
+        qw_ref[...] = mm(q[0:rows, :], w) * scale
 
     def fresh():
-        fit = mm(qw_ref[...], gf[1].reshape(K, K))
-        f_ref[...] = ypad[0:rows, K:2 * K] - fit[0:rows, :]
+        g_ref[...] = gf[1].reshape(K, K)
+        y2_ref[...] = ypad[0:rows, K:2 * K]
 
     for h in range(2):
         for j in range(ny):
@@ -660,7 +661,7 @@
         acts.append(Act(("chol", b), functools.partial(chol_block, b), after=[prev], cost=3.3, idle=True))
         prev = ("chol", b)
     acts.append(Act("basis", basis, after=[prev], cost=2.0, idle=True))
-    acts.append(Act("fresh", fresh, after=["basis", g2], cost=1.2))
+    acts.append(Act("fresh", fresh, after=["basis", g2], cost=0.3))
     for _, act in arrange(acts, 7.0, arrive):
         act.run()
     sent.append((xs.at[0], xb_ref))
@@ -685,13 +686,13 @@
     out = jax.ShapeDtypeStruct((rows, K), F32)
     return pl.pallas_call(
         functools.partial(fused_kernel, ny, nz, rows, 1.0 / leaf_rows),
-        out_shape=(out, out),
+        out_shape=(out, out, out, jax.ShapeDtypeStruct((K, K), F32)),
         in_specs=[
             pl.BlockSpec(memory_space=pltpu.SMEM),
             pl.BlockSpec(memory_space=pltpu.VMEM),
             pl.BlockSpec(memory_space=pl.ANY),
         ],
-        out_specs=[pl.BlockSpec(memory_space=pltpu.VMEM)] * 2,
+        out_specs=[pl.BlockSpec(memory_space=pltpu.VMEM)] * 4,
         scratch_shapes=[
             *slots1, *slots2,
             *[dma((2, groups(ny if s[0] == "Y" else nz))) for s in sets],
@@ -702,13 +703,29 @@
             vm((TILE, 2 * K), F32), vm((2, 2, K // 2, K), F32), vm((2, K // 2, K), F32),
             vm((2, nz, piece, K), F32), vm((2, nz - 1, piece, K), F32), vm((2, piece, K), F32),
             vm((2, max(1, ny - 1), piece, K), F32), vm((2, 2, nz, piece, K), F32),
-            vm((K, 2 * K), F32), vm((TILE, K), F32),
+            vm((K, 2 * K), F32),
             dma((ny + 1,)), dma((1,)), dma((2, ny)),
             dma((len(sets),)), dma((len(sets),)), dma((2, 5)), dma((2, 5)),
         ],
         compiler_params=pltpu.CompilerParams(
             collective_id=0, has_side_effects=True, vmem_limit_bytes=63 << 20),
     )(seeds, child_map, expanded.reshape(2, ny, chunk, block_cols))
+
+
+def finish_kernel(q_ref, y2_ref, qw_ref, g_ref, q_out, f_out):
+    q_out[...] = q_ref[...]
+    f_out[...] = y2_ref[...] - mm(qw_ref[...], g_ref[...])
+
+
+def finish(q, y2, qw, g):
+    out = jax.ShapeDtypeStruct(q.shape, F32)
+    return pl.pallas_call(
+        finish_kernel,
+        out_shape=(out, out),
+        in_specs=[pl.BlockSpec(memory_space=pltpu.VMEM)] * 4,
+        out_specs=[pl.BlockSpec(memory_space=pltpu.VMEM)] * 2,
+        compiler_params=pltpu.CompilerParams(vmem_limit_bytes=63 << 20),
+    )(q, y2, qw, g)
 
 
 def make_body(parent_rows):
@@ -718,7 +735,7 @@
         leaf_rows = parent_rows // lax.axis_size("row")
         own_rows = leaf_rows // (2 * col_count)
         expanded = expand_rows(schur_blocks[0], child_map, leaf_rows)
-        return fused(expanded, child_map, round_seeds, ny, nz, own_rows, leaf_rows)
+        return finish(*fused(expanded, child_map, round_seeds, ny, nz, own_rows, leaf_rows))
     return body
 
 

time: 112 us -> 109 us (0.973)
  local copies, waits for them, and re-layouts: 8.8 us -> 3.08 us
  Pallas kernels: 102 us -> 105 us
    unnamed x8 -> x4, local copies, waits for them, and re-layouts: 8.8 us -> 3.08 us
    pallas_call x1, Pallas kernels: 5.13 us -> 8.22 us  [expand_rows(): pl.pallas_call(expand_kernel, grid=(leaf_rows // rows,), out_shape=jax.Sh...]
    pallas_call x0 -> x1, Pallas kernels: none -> 1.95 us  [finish(): pl.pallas_call(finish_kernel, out_shape=(out, out), in_specs=[pl.BlockSpe...]
    pallas_call x1, Pallas kernels: 96.8 us -> 95.3 us  [fused(): pl.pallas_call(functools.partial(fused_kernel, ny, nz, rows, 1.0 / leaf_r...]
where the time goes in v5:
time: 109 us
  Pallas kernels  105 us (96%)
  local copies, waits for them, and re-layouts  3.08 us (3%)
    pallas_call x1, Pallas kernels, fused(): pl.pallas_call(functools.partial(fused_kernel, ny, nz, rows, 1.0 / leaf_r...  95.3 us
    pallas_call x1, Pallas kernels, expand_rows(): pl.pallas_call(expand_kernel, grid=(leaf_rows // rows,), out_shape=jax.Sh...  8.22 us
    unnamed x4, local copies, waits for them, and re-layouts  3.08 us

profile of v5, /device:TPU:1, one launch (start us, length us, event | category | flops | bytes accessed | tf_op | source)
XLA Modules:
  0.0 109.2 jit_solution(12819063135247603335)
XLA Ops:
  0.6 0.0 copy-start
  0.6 2.2 %copy-done = bf16[1,4096,512]{2,1,0:T(8,128)(2,1)S(1)} copy-done((bf16[1,4096,512]{2,1,0:T(8,128)(2,1)S(1)}, bf16[1,4096,512]{2,1,0:T(8,128)(2,1)}, u32[]{:S(2)}) %copy-start) | copy-done | bytes 4194328
  2.8 0.0 copy-start.1
  2.8 0.9 copy-done.1
  3.7 8.2 %shard_map.50 = bf16[6144,512]{1,0:T(8,128)(2,1)} custom-call(s32[2,16384]{1,0:T(2,128)S(1)} %copy-done.1, bf16[4096,512]{1,0:T(8,128)(2,1)S(1)} %bitcast.2), custom_call_target="tpu_custom_call" | custom-call | tf_op jit(solution)/shard_map/pallas_call | solution.py:141
  12.0 95.3 %shard_map.51 = (f32[96,256]{1,0:T(8,128)}, f32[96,256]{1,0:T(8,128)}, f32[96,256]{1,0:T(8,128)}, f32[256,256]{1,0:T(8,128)}) custom-call(s32[2]{0:T(128)} %seeds_ref.1, s32[2,16384]{1,0:T(2,128)} %map_ref.3, bf16[2,4,768,512]{3,2,1,0:T(8,128)(2,1)} %bitcast.3), custom_call_target="tpu_custom_call" | custom-call | tf_op jit(solution)/shard_map/pallas_call | solution.py:687
  107.3 2.0 %shard_map.52 = (f32[96,256]{1,0:T(8,128)}, f32[96,256]{1,0:T(8,128)}) custom-call(f32[96,256]{1,0:T(8,128)} %get-tuple-element.6.q_ref, f32[96,256]{1,0:T(8,128)} %get-tuple-element.7.y2_ref, f32[96,256]{1,0:T(8,128)} %get-tuple-element.8.qw_ref, f32[256,256]{1,0:T(8,128)} %get-tuple-element.9.g_ref), custom_call_target="tpu_custom_call" | custom-call | tf_op jit(solution)/shard_map/pallas_call | solution.py:722
Async XLA Ops:
  0.6 2.2 %copy-start = (bf16[1,4096,512]{2,1,0:T(8,128)(2,1)S(1)}, bf16[1,4096,512]{2,1,0:T(8,128)(2,1)}, u32[]{:S(2)}) copy-start(bf16[1,4096,512]{2,1,0:T(8,128)(2,1)} %param.3) | copy-start | bytes 12582916
  2.8 0.9 copy-start.1

commit v6 on v5

--- a/solution.py
+++ b/solution.py
@@ -103,10 +103,17 @@
     row = lax.axis_index("row")
     base = row * (e_ref.shape[0] * pl.num_programs(0))
 
+    size = STEP_TILES * TILE
+    parts = block_rows // size
+
+    def load(n):
+        rows = pl.ds(n * size, size)
+        return pltpu.make_async_copy(a_hbm.at[rows, :], a_ref.at[rows, :], a_sem.at[n])
+
     @pl.when(step == 0)
     def _():
-        load = pltpu.make_async_copy(a_hbm, a_ref, a_sem)
-        load.start()
+        for n in range(parts):
+            load(n).start()
 
         def fill(j, carry):
             at = pl.multiple_of(row * block_rows + j * TILE, TILE)
@@ -121,7 +128,12 @@
         to_scalar = pltpu.make_async_copy(sv_ref, ss_ref, sv_sem)
         to_scalar.start()
         to_scalar.wait()
-        load.wait()
+        load(0).wait()
+
+    for n in range(1, parts):
+        @pl.when(step == n - 1)
+        def _():
+            load(n).wait()
 
     for q in range(STEP_TILES):
         t = step * STEP_TILES + q
@@ -148,9 +160,9 @@
             pltpu.VMEM((block_rows, block_cols), bf),
             pltpu.VMEM((block_rows // TILE, TILE), jnp.int32), pltpu.VMEM((8, TILE), jnp.int32),
             pltpu.SMEM((8, TILE), jnp.int32),
-            pltpu.SemaphoreType.DMA(()), pltpu.SemaphoreType.DMA(()),
+            pltpu.SemaphoreType.DMA((block_rows // rows,)), pltpu.SemaphoreType.DMA(()),
         ],
-        compiler_params=pltpu.CompilerParams(vmem_limit_bytes=48 << 20),
+        compiler_params=pltpu.CompilerParams(vmem_limit_bytes=63 << 20),
     )(child_map, child_block)
 
 

time: 109 us -> 107 us (0.982)
  local copies, waits for them, and re-layouts: 3.08 us -> 0 us
  Pallas kernels: 105 us -> 107 us
    unnamed x4 -> x0, local copies, waits for them, and re-layouts: 3.08 us -> none
where the time goes in v6:
time: 107 us
  Pallas kernels  107 us (100%)
    pallas_call x1, Pallas kernels, fused(): pl.pallas_call(functools.partial(fused_kernel, ny, nz, rows, 1.0 / leaf_r...  95.4 us
    pallas_call x1, Pallas kernels, expand_rows(): pl.pallas_call(expand_kernel, grid=(leaf_rows // rows,), out_shape=jax.Sh...  9.3 us

profile of v6, /device:TPU:1, one launch (start us, length us, event | category | flops | bytes accessed | tf_op | source)
XLA Modules:
  0.0 107.3 jit_solution(4894050155405865181)
XLA Ops:
  0.6 9.3 %shard_map.50 = bf16[6144,512]{1,0:T(8,128)(2,1)} custom-call(s32[2,16384]{1,0:T(2,128)} %map_ref.3, bf16[4096,512]{1,0:T(8,128)(2,1)} %bitcast.3), custom_call_target="tpu_custom_call" | custom-call | tf_op jit(solution)/shard_map/pallas_call | solution.py:153
  9.9 95.4 %shard_map.51 = (f32[96,256]{1,0:T(8,128)}, f32[96,256]{1,0:T(8,128)}, f32[96,256]{1,0:T(8,128)}, f32[256,256]{1,0:T(8,128)}) custom-call(s32[2]{0:T(128)} %seeds_ref.1, s32[2,16384]{1,0:T(2,128)} %map_ref.3, bf16[2,4,768,512]{3,2,1,0:T(8,128)(2,1)} %bitcast.2), custom_call_target="tpu_custom_call" | custom-call | tf_op jit(solution)/shard_map/pallas_call | solution.py:699
  105.4 2.0 %shard_map.52 = (f32[96,256]{1,0:T(8,128)}, f32[96,256]{1,0:T(8,128)}) custom-call(f32[96,256]{1,0:T(8,128)} %get-tuple-element.6.q_ref, f32[96,256]{1,0:T(8,128)} %get-tuple-element.7.y2_ref, f32[96,256]{1,0:T(8,128)} %get-tuple-element.8.qw_ref, f32[256,256]{1,0:T(8,128)} %get-tuple-element.9.g_ref), custom_call_target="tpu_custom_call" | custom-call | tf_op jit(solution)/shard_map/pallas_call | solution.py:734

commit v7 on v6

--- a/solution.py
+++ b/solution.py
@@ -92,7 +92,7 @@
     return order
 
 
-STEP_TILES = 4
+STEP_TILES = 8
 
 
 def expand_kernel(map_ref, a_hbm, e_ref, a_ref, m2_ref, sv_ref, ss_ref, a_sem, sv_sem):

time: 107 us -> 105 us (0.981)
  Pallas kernels: 107 us -> 104 us
    pallas_call x1, Pallas kernels: 9.3 us -> 7.39 us  [expand_rows(): pl.pallas_call(expand_kernel, grid=(leaf_rows // rows,), out_shape=jax.Sh...]
where the time goes in v7:
time: 105 us
  Pallas kernels  104 us (99%)
    pallas_call x1, Pallas kernels, fused(): pl.pallas_call(functools.partial(fused_kernel, ny, nz, rows, 1.0 / leaf_r...  94.7 us
    pallas_call x1, Pallas kernels, expand_rows(): pl.pallas_call(expand_kernel, grid=(leaf_rows // rows,), out_shape=jax.Sh...  7.39 us

profile of v7, /device:TPU:1, one launch (start us, length us, event | category | flops | bytes accessed | tf_op | source)
XLA Modules:
  0.0 104.7 jit_solution(10222775009758412044)
XLA Ops:
  0.6 7.4 %shard_map.50 = bf16[6144,512]{1,0:T(8,128)(2,1)} custom-call(s32[2,16384]{1,0:T(2,128)} %map_ref.3, bf16[4096,512]{1,0:T(8,128)(2,1)} %bitcast.3), custom_call_target="tpu_custom_call" | custom-call | tf_op jit(solution)/shard_map/pallas_call | solution.py:153
  8.0 94.7 %shard_map.51 = (f32[96,256]{1,0:T(8,128)}, f32[96,256]{1,0:T(8,128)}, f32[96,256]{1,0:T(8,128)}, f32[256,256]{1,0:T(8,128)}) custom-call(s32[2]{0:T(128)} %seeds_ref.1, s32[2,16384]{1,0:T(2,128)} %map_ref.3, bf16[2,4,768,512]{3,2,1,0:T(8,128)(2,1)} %bitcast.2), custom_call_target="tpu_custom_call" | custom-call | tf_op jit(solution)/shard_map/pallas_call | solution.py:699
  102.8 2.0 %shard_map.52 = (f32[96,256]{1,0:T(8,128)}, f32[96,256]{1,0:T(8,128)}) custom-call(f32[96,256]{1,0:T(8,128)} %get-tuple-element.6.q_ref, f32[96,256]{1,0:T(8,128)} %get-tuple-element.7.y2_ref, f32[96,256]{1,0:T(8,128)} %get-tuple-element.8.qw_ref, f32[256,256]{1,0:T(8,128)} %get-tuple-element.9.g_ref), custom_call_target="tpu_custom_call" | custom-call | tf_op jit(solution)/shard_map/pallas_call | solution.py:734
